TPU v7x, 512 devices: a whole 4x4x16 slice. The times are simulated.
512 devices in a mesh: section: 16 (over y, x_lo, core), dp: 32 (over x_hi, z).
Axes of the slice: x: 4 (x_hi: 2, x_lo: 2; x = x_hi * 2 + x_lo), y: 4, z: 16, core: 2. Of those that a mesh axis runs over, the one named last changes fastest.
Arguments:
- acts: bfloat16 [16, 2, 4096, 512], P('section', None, 'dp'), may hold values from -12 to 12
- weights: bfloat16 [16, 512, 512], P('section'), may hold values from -0.25 to 0.25
- cot_last: bfloat16 [2, 4096, 512], P(None, 'dp'), may hold values from -1.796875 to 1.796875
Outputs:
- input_cots: bfloat16 [16, 2, 4096, 512], P('section', None, 'dp')
- update: float32 [16, 512, 512], P('section')
All inputs are finite; a program needn't handle non-finite values.
Results may differ from a plain program's by a relative error of at most 0.025.
Values may be sent and summed in bfloat16 or wider, within the bound.
A program may use at most 64 MiB of HBM per device.

v0:
```python
import jax
import jax.numpy as jnp
from jax import lax
from jax.sharding import PartitionSpec as P

NS_STEPS = 3


def shifted(block, axis, distance):
    devices = range(lax.axis_size(axis))
    route = [(i - distance, i) for i in devices if i - distance in devices]
    return lax.ppermute(block, axis, route)


def silu_slope(pre):
    sig = jax.nn.sigmoid(pre)
    return sig * (1.0 + pre * (1.0 - sig))


def moment(left, right):
    return lax.dot_general(
        left, right, (((0,), (0,)), ((), ())), preferred_element_type=jnp.float32
    )


def newton(matrix):
    eye = jnp.eye(matrix.shape[0], dtype=jnp.float32)
    approx = eye / jnp.sqrt(jnp.sum(matrix * matrix))
    for step in range(NS_STEPS):
        inner = jnp.dot(matrix, approx, precision=lax.Precision.HIGHEST)
        approx = 2.0 * approx - jnp.dot(approx, inner, precision=lax.Precision.HIGHEST)
    return approx


def body(acts, weights, cot_last):
    sections = lax.axis_size("section")
    here = lax.axis_index("section")
    weight = weights[0]
    local = acts[0]
    micro, rows, width = local.shape
    flat = local.reshape(micro * rows, width)
    count = micro * rows * lax.axis_size("dp")
    eye = jnp.eye(width, dtype=jnp.float32)

    def tick(turn, carry):
        incoming, dh_store, dx_store = carry
        slot = turn - (sections - 1 - here)
        active = jnp.logical_and(slot >= 0, slot < micro)
        index = jnp.clip(slot, 0, micro - 1)
        inputs = lax.dynamic_index_in_dim(local, index, 0, keepdims=False)
        arriving = lax.dynamic_index_in_dim(cot_last, index, 0, keepdims=False)
        upstream = jnp.where(here == sections - 1, arriving, incoming)
        pre = jnp.dot(inputs, weight, preferred_element_type=jnp.float32)
        slope_dh = (upstream.astype(jnp.float32) * silu_slope(pre)).astype(jnp.bfloat16)
        back = lax.dot_general(
            slope_dh, weight, (((1,), (1,)), ((), ())), preferred_element_type=jnp.float32
        )
        result = (upstream.astype(jnp.float32) + back).astype(jnp.bfloat16)
        old_dh = lax.dynamic_index_in_dim(dh_store, index, 0, keepdims=False)
        old_dx = lax.dynamic_index_in_dim(dx_store, index, 0, keepdims=False)
        dh_store = lax.dynamic_update_index_in_dim(
            dh_store, jnp.where(active, slope_dh, old_dh), index, 0
        )
        dx_store = lax.dynamic_update_index_in_dim(
            dx_store, jnp.where(active, result, old_dx), index, 0
        )
        incoming = shifted(result, "section", -1)
        return (incoming, dh_store, dx_store)

    start = (
        jnp.zeros((rows, width), jnp.bfloat16),
        jnp.zeros((micro, rows, width), jnp.bfloat16),
        jnp.zeros((micro, rows, width), jnp.bfloat16),
    )
    finished = lax.fori_loop(0, sections + micro - 1, tick, start)
    dh_flat = finished[1].reshape(micro * rows, width)
    act_sum, out_sum, grad_sum = lax.psum(
        (moment(flat, flat), moment(dh_flat, dh_flat), moment(flat, dh_flat)), "dp"
    )
    act_factor = act_sum / count + 0.01 * eye
    out_factor = out_sum / count + 0.01 * eye
    act_inv = newton(act_factor)
    out_inv = newton(out_factor)
    update = jnp.dot(
        jnp.dot(act_inv, grad_sum, precision=lax.Precision.HIGHEST),
        out_inv,
        precision=lax.Precision.HIGHEST,
    )
    return (finished[2][None], update[None])


def solution(mesh):
    placed = (P("section", None, "dp", None), P("section", None, None), P(None, "dp", None))
    return jax.shard_map(
        body,
        mesh=mesh,
        in_specs=placed,
        out_specs=(P("section", None, "dp", None), P("section", None, None)),
        check_vma=False,
    )
```

profile of v0, /device:TPU:8, one launch (start us, length us, event | category | flops | bytes accessed | tf_op | source)
XLA Modules:
  0.0 500.6 jit_solution(15149565637773788097)
XLA Ops:
  7.2 2.4 convolution_bitcast_fusion.2
  9.7 0.9 copy-done
  10.7 132.0 %while.19 = (s32[]{:T(128)}, bf16[128,512]{1,0:T(8,128)(2,1)S(1)}, bf16[2,128,512]{2,1,0:T(8,128)(2,1)S(1)}, bf16[2,128,512]{2,1,0:T(8,128)(2,1)S(1)}, pred[]{:T...) while((s32[]{:T(128)}, bf16[128,512]{1,0:T(8,128)(2,1)S(1)}, ...), condition=%wide.region_1.2_spmd, body=%wide.region_0.1_spmd.sunk | while | flops 135331840 | bytes 3671777 | solution.py:75
  10.7 0.3 bitcast_dynamic-update-slice_fusion.4
  11.4 2.7 collective-permute-start
  14.1 2.5 collective-permute-done
  16.6 0.3 bitcast_dynamic-update-slice_fusion.4
  17.3 4.7 collective-permute-start
  22.0 2.5 collective-permute-done
  24.5 0.3 bitcast_dynamic-update-slice_fusion.4
  25.2 4.7 collective-permute-start
  29.9 2.5 collective-permute-done
  32.4 0.3 bitcast_dynamic-update-slice_fusion.4
  33.0 4.7 collective-permute-start
  37.7 2.5 collective-permute-done
  40.3 0.3 bitcast_dynamic-update-slice_fusion.4
  40.9 4.7 collective-permute-start
  45.6 2.5 collective-permute-done
  48.1 0.3 bitcast_dynamic-update-slice_fusion.4
  48.8 4.7 collective-permute-start
  53.5 2.5 collective-permute-done
  56.0 0.3 bitcast_dynamic-update-slice_fusion.4
  56.7 4.7 collective-permute-start
  61.4 2.5 collective-permute-done
  63.9 0.3 bitcast_dynamic-update-slice_fusion.4
  64.6 4.7 collective-permute-start
  69.3 2.5 collective-permute-done
  72.5 4.7 collective-permute-start
  77.2 2.5 collective-permute-done
  80.3 4.7 collective-permute-start
  85.0 2.5 collective-permute-done
  88.2 4.7 collective-permute-start
  92.9 2.5 collective-permute-done
  96.1 4.7 collective-permute-start
  100.8 2.5 collective-permute-done
  104.0 4.7 collective-permute-start
  108.7 2.5 collective-permute-done
  111.9 4.7 collective-permute-start
  116.6 2.5 collective-permute-done
  119.8 4.7 collective-permute-start
  124.4 2.5 collective-permute-done
  127.0 0.3 bitcast_dynamic-update-slice_fusion.4
  127.6 4.7 collective-permute-start
  132.3 2.5 collective-permute-done
  135.5 4.7 collective-permute-start
  140.2 2.5 collective-permute-done
  142.7 1.3 convolution_bitcast_fusion
  144.0 1.3 convolution_bitcast_fusion.1
  145.3 317.2 %all-reduce.3.cloned.1.call-done = (f32[512,512]{1,0:T(8,128)}, f32[512,512]{0,1:T(8,128)}, f32[512,512]{1,0:T(8,128)}) async-done(((f32[512,512]{1,0:T(8,128)}, f32[512,512]{0,1:T(8,128)}, f32[512,512]{1,0:T(8,128)}), (f32[512,512]{1,0:T(8,128)}, f32[512,512]{0,1:T(8,128)}, f32[512,512]{1,0:T(8,128)})) %all-reduce.3.cloned.1.call-update) | async-done | bytes 3145744 | tf_op jit(solution)/shard_map/psum | solution.py:77
  462.5 2.6 multiply_reduce_fusion
  466.5 1.8 fusion.10
  468.3 1.8 fusion.19
  470.1 1.9 fusion.33
  472.0 1.8 convolution_subtract_fusion.1
  473.9 1.9 fusion.32
  475.8 1.8 convolution_subtract_fusion
  477.6 2.0 fusion.14
  479.7 1.8 fusion.16
  481.5 1.9 fusion.31
  483.4 1.8 convolution_subtract_fusion.3
  485.2 1.9 fusion.30
  487.2 1.9 convolution_subtract_fusion.2
  489.0 1.9 fusion.55
  490.9 2.8 convolution_bitcast_fusion.3
  (60 shorter events, 8.5 us)
Async XLA Ops:
  7.2 455.4 %all-reduce.3.cloned.1.call-start = ((), (), s32[]{:S(2)}) async-start(), calls=%async_computation | async-start | bytes 6291456 | tf_op jit(solution)/shard_map/psum | solution.py:77
  7.2 2.5 copy-start.4
  7.2 2.5 copy-start.6
  9.6 1.0 copy-start
  11.4 5.2 %collective-permute-start = (bf16[128,512]{1,0:T(8,128)(2,1)S(1)}, bf16[128,512]{1,0:T(8,128)(2,1)S(1)}, u32[]{:S(2)}, u32[]{:S(2)}) collective-permute-start(bf16[128,512]{1,0:T(8,128)(2,1)S(1)} %get-tuple-element.294), channel_id=1, source_target_pairs={{32,0},{64,32},{96,64},{128,96},{160,128},{192,160},{224,192},{256... | collective-permute-start | bytes 393224 | tf_op jit(solution)/shard_map/while/body/eval_jaxpr/ppermute | solution.py:12
  17.3 7.2 %collective-permute-start = (bf16[128,512]{1,0:T(8,128)(2,1)S(1)}, bf16[128,512]{1,0:T(8,128)(2,1)S(1)}, u32[]{:S(2)}, u32[]{:S(2)}) collective-permute-start(bf16[128,512]{1,0:T(8,128)(2,1)S(1)} %get-tuple-element.294), channel_id=1, source_target_pairs={{32,0},{64,32},{96,64},{128,96},{160,128},{192,160},{224,192},{256... | collective-permute-start | bytes 393224 | tf_op jit(solution)/shard_map/while/body/eval_jaxpr/ppermute | solution.py:12
  25.2 7.2 %collective-permute-start = (bf16[128,512]{1,0:T(8,128)(2,1)S(1)}, bf16[128,512]{1,0:T(8,128)(2,1)S(1)}, u32[]{:S(2)}, u32[]{:S(2)}) collective-permute-start(bf16[128,512]{1,0:T(8,128)(2,1)S(1)} %get-tuple-element.294), channel_id=1, source_target_pairs={{32,0},{64,32},{96,64},{128,96},{160,128},{192,160},{224,192},{256... | collective-permute-start | bytes 393224 | tf_op jit(solution)/shard_map/while/body/eval_jaxpr/ppermute | solution.py:12
  33.0 7.2 %collective-permute-start = (bf16[128,512]{1,0:T(8,128)(2,1)S(1)}, bf16[128,512]{1,0:T(8,128)(2,1)S(1)}, u32[]{:S(2)}, u32[]{:S(2)}) collective-permute-start(bf16[128,512]{1,0:T(8,128)(2,1)S(1)} %get-tuple-element.294), channel_id=1, source_target_pairs={{32,0},{64,32},{96,64},{128,96},{160,128},{192,160},{224,192},{256... | collective-permute-start | bytes 393224 | tf_op jit(solution)/shard_map/while/body/eval_jaxpr/ppermute | solution.py:12
  40.9 7.2 %collective-permute-start = (bf16[128,512]{1,0:T(8,128)(2,1)S(1)}, bf16[128,512]{1,0:T(8,128)(2,1)S(1)}, u32[]{:S(2)}, u32[]{:S(2)}) collective-permute-start(bf16[128,512]{1,0:T(8,128)(2,1)S(1)} %get-tuple-element.294), channel_id=1, source_target_pairs={{32,0},{64,32},{96,64},{128,96},{160,128},{192,160},{224,192},{256... | collective-permute-start | bytes 393224 | tf_op jit(solution)/shard_map/while/body/eval_jaxpr/ppermute | solution.py:12
  48.8 7.2 %collective-permute-start = (bf16[128,512]{1,0:T(8,128)(2,1)S(1)}, bf16[128,512]{1,0:T(8,128)(2,1)S(1)}, u32[]{:S(2)}, u32[]{:S(2)}) collective-permute-start(bf16[128,512]{1,0:T(8,128)(2,1)S(1)} %get-tuple-element.294), channel_id=1, source_target_pairs={{32,0},{64,32},{96,64},{128,96},{160,128},{192,160},{224,192},{256... | collective-permute-start | bytes 393224 | tf_op jit(solution)/shard_map/while/body/eval_jaxpr/ppermute | solution.py:12
  56.7 7.2 %collective-permute-start = (bf16[128,512]{1,0:T(8,128)(2,1)S(1)}, bf16[128,512]{1,0:T(8,128)(2,1)S(1)}, u32[]{:S(2)}, u32[]{:S(2)}) collective-permute-start(bf16[128,512]{1,0:T(8,128)(2,1)S(1)} %get-tuple-element.294), channel_id=1, source_target_pairs={{32,0},{64,32},{96,64},{128,96},{160,128},{192,160},{224,192},{256... | collective-permute-start | bytes 393224 | tf_op jit(solution)/shard_map/while/body/eval_jaxpr/ppermute | solution.py:12
  64.6 7.2 %collective-permute-start = (bf16[128,512]{1,0:T(8,128)(2,1)S(1)}, bf16[128,512]{1,0:T(8,128)(2,1)S(1)}, u32[]{:S(2)}, u32[]{:S(2)}) collective-permute-start(bf16[128,512]{1,0:T(8,128)(2,1)S(1)} %get-tuple-element.294), channel_id=1, source_target_pairs={{32,0},{64,32},{96,64},{128,96},{160,128},{192,160},{224,192},{256... | collective-permute-start | bytes 393224 | tf_op jit(solution)/shard_map/while/body/eval_jaxpr/ppermute | solution.py:12
  72.5 7.2 %collective-permute-start = (bf16[128,512]{1,0:T(8,128)(2,1)S(1)}, bf16[128,512]{1,0:T(8,128)(2,1)S(1)}, u32[]{:S(2)}, u32[]{:S(2)}) collective-permute-start(bf16[128,512]{1,0:T(8,128)(2,1)S(1)} %get-tuple-element.294), channel_id=1, source_target_pairs={{32,0},{64,32},{96,64},{128,96},{160,128},{192,160},{224,192},{256... | collective-permute-start | bytes 393224 | tf_op jit(solution)/shard_map/while/body/eval_jaxpr/ppermute | solution.py:12
  80.3 7.2 %collective-permute-start = (bf16[128,512]{1,0:T(8,128)(2,1)S(1)}, bf16[128,512]{1,0:T(8,128)(2,1)S(1)}, u32[]{:S(2)}, u32[]{:S(2)}) collective-permute-start(bf16[128,512]{1,0:T(8,128)(2,1)S(1)} %get-tuple-element.294), channel_id=1, source_target_pairs={{32,0},{64,32},{96,64},{128,96},{160,128},{192,160},{224,192},{256... | collective-permute-start | bytes 393224 | tf_op jit(solution)/shard_map/while/body/eval_jaxpr/ppermute | solution.py:12
  88.2 7.2 %collective-permute-start = (bf16[128,512]{1,0:T(8,128)(2,1)S(1)}, bf16[128,512]{1,0:T(8,128)(2,1)S(1)}, u32[]{:S(2)}, u32[]{:S(2)}) collective-permute-start(bf16[128,512]{1,0:T(8,128)(2,1)S(1)} %get-tuple-element.294), channel_id=1, source_target_pairs={{32,0},{64,32},{96,64},{128,96},{160,128},{192,160},{224,192},{256... | collective-permute-start | bytes 393224 | tf_op jit(solution)/shard_map/while/body/eval_jaxpr/ppermute | solution.py:12
  96.1 7.2 %collective-permute-start = (bf16[128,512]{1,0:T(8,128)(2,1)S(1)}, bf16[128,512]{1,0:T(8,128)(2,1)S(1)}, u32[]{:S(2)}, u32[]{:S(2)}) collective-permute-start(bf16[128,512]{1,0:T(8,128)(2,1)S(1)} %get-tuple-element.294), channel_id=1, source_target_pairs={{32,0},{64,32},{96,64},{128,96},{160,128},{192,160},{224,192},{256... | collective-permute-start | bytes 393224 | tf_op jit(solution)/shard_map/while/body/eval_jaxpr/ppermute | solution.py:12
  104.0 7.2 %collective-permute-start = (bf16[128,512]{1,0:T(8,128)(2,1)S(1)}, bf16[128,512]{1,0:T(8,128)(2,1)S(1)}, u32[]{:S(2)}, u32[]{:S(2)}) collective-permute-start(bf16[128,512]{1,0:T(8,128)(2,1)S(1)} %get-tuple-element.294), channel_id=1, source_target_pairs={{32,0},{64,32},{96,64},{128,96},{160,128},{192,160},{224,192},{256... | collective-permute-start | bytes 393224 | tf_op jit(solution)/shard_map/while/body/eval_jaxpr/ppermute | solution.py:12
  111.9 7.2 %collective-permute-start = (bf16[128,512]{1,0:T(8,128)(2,1)S(1)}, bf16[128,512]{1,0:T(8,128)(2,1)S(1)}, u32[]{:S(2)}, u32[]{:S(2)}) collective-permute-start(bf16[128,512]{1,0:T(8,128)(2,1)S(1)} %get-tuple-element.294), channel_id=1, source_target_pairs={{32,0},{64,32},{96,64},{128,96},{160,128},{192,160},{224,192},{256... | collective-permute-start | bytes 393224 | tf_op jit(solution)/shard_map/while/body/eval_jaxpr/ppermute | solution.py:12
  119.8 7.2 %collective-permute-start = (bf16[128,512]{1,0:T(8,128)(2,1)S(1)}, bf16[128,512]{1,0:T(8,128)(2,1)S(1)}, u32[]{:S(2)}, u32[]{:S(2)}) collective-permute-start(bf16[128,512]{1,0:T(8,128)(2,1)S(1)} %get-tuple-element.294), channel_id=1, source_target_pairs={{32,0},{64,32},{96,64},{128,96},{160,128},{192,160},{224,192},{256... | collective-permute-start | bytes 393224 | tf_op jit(solution)/shard_map/while/body/eval_jaxpr/ppermute | solution.py:12
  127.6 7.2 %collective-permute-start = (bf16[128,512]{1,0:T(8,128)(2,1)S(1)}, bf16[128,512]{1,0:T(8,128)(2,1)S(1)}, u32[]{:S(2)}, u32[]{:S(2)}) collective-permute-start(bf16[128,512]{1,0:T(8,128)(2,1)S(1)} %get-tuple-element.294), channel_id=1, source_target_pairs={{32,0},{64,32},{96,64},{128,96},{160,128},{192,160},{224,192},{256... | collective-permute-start | bytes 393224 | tf_op jit(solution)/shard_map/while/body/eval_jaxpr/ppermute | solution.py:12
  135.5 7.2 %collective-permute-start = (bf16[128,512]{1,0:T(8,128)(2,1)S(1)}, bf16[128,512]{1,0:T(8,128)(2,1)S(1)}, u32[]{:S(2)}, u32[]{:S(2)}) collective-permute-start(bf16[128,512]{1,0:T(8,128)(2,1)S(1)} %get-tuple-element.294), channel_id=1, source_target_pairs={{32,0},{64,32},{96,64},{128,96},{160,128},{192,160},{224,192},{256... | collective-permute-start | bytes 393224 | tf_op jit(solution)/shard_map/while/body/eval_jaxpr/ppermute | solution.py:12
  142.7 1.3 copy-start.3
  462.5 3.9 copy-start.2
  475.8 1.9 copy-start.1
  487.1 1.9 copy-start.5
Sparse Core Ops, SparseCore 0:
  145.5 317.0 all-reduce.2
where the time goes:
time: 501 us
  waiting for transfers between devices  360 us (72%)
  starting transfers between devices  77.7 us (16%)
  matrix products  43.2 us (9%)
  between operations  15.6 us (3%)
    psum x1, waiting for transfers between devices, body(): lax.psum((moment(flat, flat), moment(dh_flat, dh_flat), moment(flat, dh_f...  317 us
    ppermute x17, starting transfers between devices, shifted(): return lax.ppermute(block, axis, route)  77.6 us
    ppermute x17, waiting for transfers between devices, shifted(): return lax.ppermute(block, axis, route)  42.4 us
    dot_general x6, matrix products, newton(): inner = jnp.dot(matrix, approx, precision=lax.Precision.HIGHEST)  11.4 us
    dot_general x6, matrix products, newton(): jnp.dot(approx, inner, precision=lax.Precision.HIGHEST)  11 us
  transfers between devices with their start and end apart: 18, of which 18 were waited for; matrix products, arithmetic and copies ran while one was open for 0% of the time, Pallas kernels for 0%

commit v1 on v0

v1 whole, which is shorter than its diff:
```python
import functools

import jax
import jax.numpy as jnp
from jax import lax
from jax.experimental import pallas as pl
from jax.experimental.pallas import tpu as pltpu
from jax.sharding import PartitionSpec as P

MESH = pl.DeviceIdType.MESH
T = 128
SUB = 2


def dot(a, b):
    return jnp.dot(a, b, preferred_element_type=jnp.float32)


def kernel(
    sections, rings, size,
    acts_ref, w_ref, cot_ref, dx_ref, up_ref,
    slope, xt, dyin, dh, own, stage, rbuf, red, xs, xr, full, tb, ub, zb,
    c_send, c_recv, r_send, r_recv, x_sem, g_send, g_recv,
):
    s = lax.axis_index("section")
    p = lax.axis_index("dp")
    z, ring = lax.rem(p, size), p // size
    base = ring * size
    up = (s, base + lax.rem(z + 1, size))
    down = (s, base + lax.rem(z + size - 1, size))
    over = (s, lax.rem(p + size, rings * size))
    width = w_ref.shape[1]
    nb = width // T
    half = size // 2
    piece = own.shape[0] // size
    sub = piece // SUB
    micro, rows = acts_ref.shape[1], acts_ref.shape[2]
    count = micro * rows * rings * size

    barrier = pltpu.get_barrier_semaphore()
    for peer in (up, down, over, (lax.rem(s + 1, sections), p)):
        pl.semaphore_signal(barrier, inc=1, device_id=peer, device_id_type=MESH)

    for m in range(micro):
        pre = dot(acts_ref[0, m], w_ref[0])
        sig = 1.0 / (1.0 + jnp.exp(-pre))
        slope[m] = sig * (1.0 + pre * (1.0 - sig))

    def prepare():
        x = acts_ref[0].reshape(micro * rows, width)
        xt[...] = x.T
        at = 0
        for i in range(nb):
            prod = dot(xt[i * T:(i + 1) * T, :], x[:, i * T:])
            for j in range(nb - i):
                own[pl.ds((at + j) * T, T), :] = prod[:, j * T:(j + 1) * T]
            at += nb - i

    @pl.when(s < sections - 1)
    def _():
        prepare()

    pl.semaphore_wait(barrier, 4)

    def chain_copy(m):
        return pltpu.make_async_remote_copy(
            src_ref=dx_ref.at[0, m], dst_ref=dyin.at[m],
            send_sem=c_send.at[m], recv_sem=c_recv.at[m],
            device_id=(s - 1, p), device_id_type=MESH,
        )

    @pl.when(s == sections - 1)
    def _():
        dyin[...] = cot_ref[...]

    for m in range(micro):
        @pl.when(s < sections - 1)
        def _():
            chain_copy(m).wait_recv()
        dy = dyin[m].astype(jnp.float32)
        part = (dy * slope[m]).astype(jnp.bfloat16)
        dh[m * rows:(m + 1) * rows, :] = part
        back = lax.dot_general(
            part, w_ref[0], (((1,), (1,)), ((), ())), preferred_element_type=jnp.float32
        )
        dx_ref[0, m] = (dy + back).astype(jnp.bfloat16)

        @pl.when(s > 0)
        def _():
            chain_copy(m).start()

    @pl.when(s == sections - 1)
    def _():
        prepare()

    ntri = nb * (nb + 1) // 2
    d = dh[...]
    dt = d.T
    at = ntri
    for i in range(nb):
        prod = dot(dt[i * T:(i + 1) * T, :], d[:, i * T:])
        for j in range(nb - i):
            own[pl.ds((at + j) * T, T), :] = prod[:, j * T:(j + 1) * T]
        at += nb - i
    for i in range(nb):
        prod = dot(xt[i * T:(i + 1) * T, :], d)
        for j in range(nb):
            own[pl.ds((at + j) * T, T), :] = prod[:, j * T:(j + 1) * T]
        at += nb

    def rows_of(chunk, k):
        return pl.ds(pl.multiple_of(chunk * piece + k * sub, 16), sub)

    def ring_copy(way, t, k):
        return pltpu.make_async_remote_copy(
            src_ref=stage.at[way, t, k], dst_ref=rbuf.at[way, t, k],
            send_sem=r_send.at[way, t, k], recv_sem=r_recv.at[way, t, k],
            device_id=(up, down)[way], device_id_type=MESH,
        )

    def ring_send(way, t, k, first):
        chunk = lax.rem(z + half - t if way == 0 else z + half + t, size)
        value = own[rows_of(chunk, k), :]
        if not first:
            ring_copy(way, t - 1, k).wait_recv()
            value = value + rbuf[way, t - 1, k].astype(jnp.float32)
        stage[way, t, k] = value.astype(jnp.bfloat16)
        ring_copy(way, t, k).start()

    for k in range(SUB):
        ring_send(0, 0, k, True)
        ring_send(1, 1, k, True)
    for k in range(SUB):
        ring_send(0, 1, k, False)

    def ring_step(t, carry):
        for k in range(SUB):
            for way in range(2):
                ring_send(way, t, k, False)
        return carry

    lax.fori_loop(2, half, ring_step, 0)

    def over_copy(k):
        return pltpu.make_async_remote_copy(
            src_ref=xs.at[k], dst_ref=xr.at[k], send_sem=x_sem.at[0, k],
            recv_sem=x_sem.at[1, k], device_id=over, device_id_type=MESH,
        )

    for k in range(SUB):
        value = own[rows_of(z, k), :]
        for way in range(2):
            ring_copy(way, half - 1, k).wait_recv()
            value = value + rbuf[way, half - 1, k].astype(jnp.float32)
        xs[k] = value.astype(jnp.bfloat16)
        over_copy(k).start()

    def gather_copy(way, t, k):
        chunk = lax.rem(z + size - t if way == 0 else z + t, size)
        return pltpu.make_async_remote_copy(
            src_ref=red.at[rows_of(chunk, k), :], dst_ref=red.at[rows_of(chunk, k), :],
            send_sem=g_send.at[way, t, k], recv_sem=g_recv.at[way, t, k],
            device_id=(up, down)[way], device_id_type=MESH,
        )

    def arrived(way, t, k):
        chunk = lax.rem(z + 2 * size - 1 - t if way == 0 else z + 1 + t, size)
        return pltpu.make_async_remote_copy(
            src_ref=red.at[rows_of(chunk, k), :], dst_ref=red.at[rows_of(chunk, k), :],
            send_sem=g_send.at[way, t, k], recv_sem=g_recv.at[way, t, k],
            device_id=(up, down)[way], device_id_type=MESH,
        )

    for k in range(SUB):
        over_copy(k).wait_recv()
        total = xs[k].astype(jnp.float32) + xr[k].astype(jnp.float32)
        red[rows_of(z, k), :] = total.astype(jnp.bfloat16)
        for way in range(2):
            gather_copy(way, 0, k).start()

    def gather_step(t, carry):
        for k in range(SUB):
            for way in range(2):
                arrived(way, t - 1, k).wait_recv()
                gather_copy(way, t, k).start()
        return carry

    lax.fori_loop(1, half - 1, gather_step, 0)
    for k in range(SUB):
        arrived(0, half - 2, k).wait_recv()
        gather_copy(0, half - 1, k).start()
    for k in range(SUB):
        arrived(1, half - 2, k).wait_recv()
        arrived(0, half - 1, k).wait_recv()

    def unpack(at, side):
        for i in range(nb):
            for j in range(i, nb):
                block = red[pl.ds(at * T, T), :].astype(jnp.float32) / count
                if i == j:
                    row = lax.broadcasted_iota(jnp.int32, (T, T), 0)
                    col = lax.broadcasted_iota(jnp.int32, (T, T), 1)
                    block = block + jnp.where(row == col, 0.01, 0.0)
                    full[i * T:(i + 1) * T, j * T:(j + 1) * T] = block
                else:
                    full[i * T:(i + 1) * T, j * T:(j + 1) * T] = block
                    full[j * T:(j + 1) * T, i * T:(i + 1) * T] = block.T
                at += 1
        m = full[...]
        inv = 1.0 / jnp.sqrt(jnp.sum(m * m, keepdims=True))
        tb[0] = (m * inv).astype(jnp.bfloat16)
        for h in range(2):
            r = slice(h * (width // 2), (h + 1) * (width // 2))
            t = full[r, :] * inv
            ub[0, r, :] = 2.0 * t - dot(tb[0, r, :], tb[0])
        tb[1] = ub[0].astype(jnp.bfloat16)
        for h in range(2):
            r = slice(h * (width // 2), (h + 1) * (width // 2))
            u = ub[0, r, :]
            ub[1, r, :] = 2.0 * u - dot(tb[1, r, :], tb[1])
        tb[2] = ub[1].astype(jnp.bfloat16)
        for h in range(2):
            r = slice(h * (width // 2), (h + 1) * (width // 2))
            y = 2.0 * (full[r, :] * inv + ub[0, r, :]) - dot(tb[0, r, :], tb[1])
            zz = 4.0 * ub[1, r, :] + 2.0 * y - dot(y.astype(jnp.bfloat16), tb[2])
            zb[side, r, :] = zz.astype(jnp.bfloat16)
        return inv

    inv_a = unpack(0, 0)
    inv_o = unpack(ntri, 1)
    for i in range(nb):
        for j in range(nb):
            block = red[pl.ds((2 * ntri + i * nb + j) * T, T), :]
            tb[0, i * T:(i + 1) * T, j * T:(j + 1) * T] = block
    scale = inv_a * inv_o
    for h in range(2):
        r = slice(h * (width // 2), (h + 1) * (width // 2))
        full[r, :] = 8.0 * tb[0, r, :].astype(jnp.float32) - dot(tb[0, r, :], zb[1])
    tb[1] = full[...].astype(jnp.bfloat16)
    for h in range(2):
        r = slice(h * (width // 2), (h + 1) * (width // 2))
        up_ref[0, r, :] = (8.0 * full[r, :] - dot(zb[0, r, :], tb[1])) * scale

    @pl.when(s > 0)
    def _():
        for m in range(micro):
            chain_copy(m).wait_send()

    def drain(t, carry):
        for k in range(SUB):
            ring_copy(0, t, k).wait_send()
            gather_copy(0, t, k).wait_send()
        return carry

    lax.fori_loop(0, half, drain, 0)

    def drain_down(t, carry):
        for k in range(SUB):
            ring_copy(1, t + 1, k).wait_send()
            gather_copy(1, t, k).wait_send()
        return carry

    lax.fori_loop(0, half - 1, drain_down, 0)
    for k in range(SUB):
        over_copy(k).wait_send()


def body(rings, acts, weights, cot_last):
    sections = lax.axis_size("section")
    size = lax.axis_size("dp") // rings
    _, micro, rows, width = acts.shape
    nb = width // T
    total = (nb * (nb + 1) + nb * nb) * T
    piece = total // size
    half = size // 2
    vmem = pl.BlockSpec(memory_space=pltpu.VMEM)
    bf16, f32 = jnp.bfloat16, jnp.float32
    dma = pltpu.SemaphoreType.DMA
    return pl.pallas_call(
        functools.partial(kernel, sections, rings, size),
        name="relay",
        out_shape=(
            jax.ShapeDtypeStruct((1, micro, rows, width), bf16),
            jax.ShapeDtypeStruct((1, width, width), f32),
        ),
        in_specs=[vmem] * 3,
        out_specs=(vmem, vmem),
        scratch_shapes=[
            pltpu.VMEM((micro, rows, width), f32),
            pltpu.VMEM((width, micro * rows), bf16),
            pltpu.VMEM((micro, rows, width), bf16),
            pltpu.VMEM((micro * rows, width), bf16),
            pltpu.VMEM((total, T), f32),
            pltpu.VMEM((2, half, SUB, piece // SUB, T), bf16),
            pltpu.VMEM((2, half, SUB, piece // SUB, T), bf16),
            pltpu.VMEM((total, T), bf16),
            pltpu.VMEM((SUB, piece // SUB, T), bf16),
            pltpu.VMEM((SUB, piece // SUB, T), bf16),
            pltpu.VMEM((width, width), f32),
            pltpu.VMEM((3, width, width), bf16),
            pltpu.VMEM((2, width, width), f32),
            pltpu.VMEM((2, width, width), bf16),
            dma((micro,)), dma((micro,)),
            dma((2, half, SUB)), dma((2, half, SUB)),
            dma((2, SUB)),
            dma((2, half, SUB)), dma((2, half, SUB)),
        ],
        compiler_params=pltpu.CompilerParams(
            collective_id=0, has_side_effects=True, vmem_limit_bytes=40 << 20
        ),
    )(acts, weights, cot_last)


def solution(mesh):
    placed = (P("section", None, "dp", None), P("section", None, None), P(None, "dp", None))
    return jax.shard_map(
        functools.partial(body, 2),
        mesh=mesh,
        in_specs=placed,
        out_specs=(P("section", None, "dp", None), P("section", None, None)),
        check_vma=False,
    )
```

time: 501 us -> 121 us (0.24)
  the two profiles are of different devices: /device:TPU:8 before, /device:TPU:32 now
where the time goes in v1:
time: 121 us
  Pallas kernels  115 us (95%)
  local copies, waits for them, and re-layouts  4.61 us (4%)
    pallas_call x1, Pallas kernels, body(): pl.pallas_call(functools.partial(kernel, sections, rings, size), name='re...  115 us
    unnamed x8, local copies, waits for them, and re-layouts  4.61 us

profile of v1, /device:TPU:32, one launch (start us, length us, event | category | flops | bytes accessed | tf_op | source)
XLA Modules:
  0.0 120.7 jit_solution(11568961061584732783)
XLA Ops:
  0.6 0.0 copy-start
  0.6 1.0 copy-done
  1.7 0.0 copy-start.1
  1.7 0.9 copy-done.1
  2.6 0.0 copy-start.2
  2.6 0.9 copy-done.2
  3.6 115.4 %relay.1 = (bf16[1,2,128,512]{3,2,1,0:T(8,128)(2,1)S(1)}, f32[1,512,512]{2,1,0:T(8,128)S(1)}) custom-call(bf16[1,2,128,512]{3,2,1,0:T(8,128)(2,1)S(1)} %copy-done.1, bf16[1,512,512]{2,1,0:T(8,128)(2,1)S(1)} %copy-done, bf16[2,128,512]{2,1,0:T(8,128)(2,1)S(1)} %copy-done.2), custom_call_target="tpu_custom_call" | custom-call | tf_op jit(solution)/shard_map/relay/pallas_call | solution.py:279
  119.0 0.7 copy.7
  119.7 1.0 copy.8
Async XLA Ops:
  0.6 1.0 copy-start
  1.7 0.9 copy-start.1
  2.6 0.9 copy-start.2

commit v2 on v1

v2 whole, which is shorter than its diff:
```python
import functools

import jax
import jax.numpy as jnp
from jax import lax
from jax.experimental import pallas as pl
from jax.experimental.pallas import tpu as pltpu
from jax.sharding import PartitionSpec as P

MESH = pl.DeviceIdType.MESH
T = 128
ROWS = 32


def dot(a, b):
    return jnp.dot(a, b, preferred_element_type=jnp.float32)


def pieces_of(width, size):
    nb = width // T
    tri, square = nb * (nb + 1) // 2 * T, nb * nb * T
    o, g = tri // size, square // size // 2
    return ((o, 0, 0, o), (g, o, tri, 2 * g), (g, o + g, tri + g, 2 * g))


def kernel(
    sections, rings, size,
    acts_hbm, w_hbm, cot_hbm, dx_ref, up_ref,
    x_ref, w_ref, slope, xt, dyin, dh, own, stage, rbuf, red, xs, xr,
    astage, abuf, ared, axs, axr, full, tb, ub, zb,
    in_sem, c_send, c_recv, r_send, r_recv, x_sem, g_send, g_recv,
    a_send, a_recv, b_send, b_recv, ax_sem,
):
    s = lax.axis_index("section")
    p = lax.axis_index("dp")
    z, ring = lax.rem(p, size), p // size
    base = ring * size
    up = (s, base + lax.rem(z + 1, size))
    down = (s, base + lax.rem(z + size - 1, size))
    over = (s, lax.rem(p + size, rings * size))
    width = w_ref.shape[1]
    nb = width // T
    tri = nb * (nb + 1) // 2 * T
    half = size // 2
    pieces = pieces_of(width, size)
    each = range(len(pieces))
    micro, rows = dyin.shape[0], dyin.shape[1]
    per = rows // ROWS
    count = micro * rows * rings * size
    apiece = tri // size
    f32, bf16 = jnp.float32, jnp.bfloat16

    barrier = pltpu.get_barrier_semaphore()
    for peer in (over, (lax.rem(s + 1, sections), p)):
        pl.semaphore_signal(barrier, inc=1, device_id=peer, device_id_type=MESH)

    def greet(d, carry):
        peer = (s, base + lax.rem(z + d, size))
        pl.semaphore_signal(barrier, inc=1, device_id=peer, device_id_type=MESH)
        return carry

    lax.fori_loop(1, size, greet, 0)

    get_x = pltpu.make_async_copy(acts_hbm.at[0], x_ref, in_sem.at[0])
    get_w = pltpu.make_async_copy(w_hbm.at[0], w_ref, in_sem.at[1])
    get_c = pltpu.make_async_copy(cot_hbm, dyin, in_sem.at[2])
    get_x.start()
    get_w.start()

    @pl.when(s == sections - 1)
    def _():
        get_c.start()

    get_x.wait()
    get_w.wait()

    for m in range(micro):
        pre = dot(x_ref[m], w_ref[...])
        sig = 1.0 / (1.0 + jnp.exp(-pre))
        slope[m] = sig * (1.0 + pre * (1.0 - sig))

    pl.semaphore_wait(barrier, size + 1)

    def a_copy(d):
        chunk = lax.rem(z + d, size)
        return pltpu.make_async_remote_copy(
            src_ref=astage.at[pl.ds(pl.multiple_of(chunk * apiece, 16), apiece), :],
            dst_ref=abuf.at[d], send_sem=a_send.at[d], recv_sem=a_recv.at[d],
            device_id=(s, base + chunk), device_id_type=MESH,
        )

    def b_copy(d):
        mine = ared.at[pl.ds(pl.multiple_of(z * apiece, 16), apiece), :]
        return pltpu.make_async_remote_copy(
            src_ref=mine, dst_ref=mine, send_sem=b_send.at[d], recv_sem=b_recv.at[d],
            device_id=(s, base + lax.rem(z + d, size)), device_id_type=MESH,
        )

    def b_arrived(d):
        chunk = lax.rem(z + size - d, size)
        mine = ared.at[pl.ds(pl.multiple_of(chunk * apiece, 16), apiece), :]
        return pltpu.make_async_remote_copy(
            src_ref=mine, dst_ref=mine, send_sem=b_send.at[d], recv_sem=b_recv.at[d],
            device_id=(s, base + chunk), device_id_type=MESH,
        )

    ax_copy = pltpu.make_async_remote_copy(
        src_ref=axs, dst_ref=axr, send_sem=ax_sem.at[0], recv_sem=ax_sem.at[1],
        device_id=over, device_id_type=MESH,
    )

    def both_ways(start):
        def step(i, carry):
            start(i)
            start(size - i)
            return carry

        lax.fori_loop(1, half, step, 0)
        start(half)

    def a_start():
        x = x_ref[...].reshape(micro * rows, width)
        xt[...] = x.T
        at = 0
        for i in range(nb):
            prod = dot(xt[i * T:(i + 1) * T, :], x[:, i * T:]).astype(bf16)
            for j in range(nb - i):
                astage[(at + j) * T:(at + j + 1) * T, :] = prod[:, j * T:(j + 1) * T]
            at += nb - i
        both_ways(lambda d: a_copy(d).start())

    def a_middle():
        def add(d, total):
            a_copy(d).wait_recv()
            return total + abuf[d].astype(f32)

        first = astage[pl.ds(pl.multiple_of(z * apiece, 16), apiece), :].astype(f32)
        axs[...] = lax.fori_loop(1, size, add, first).astype(bf16)
        ax_copy.start()
        ax_copy.wait_recv()
        total = axs[...].astype(f32) + axr[...].astype(f32)
        ared[pl.ds(pl.multiple_of(z * apiece, 16), apiece), :] = total.astype(bf16)
        both_ways(lambda d: b_copy(d).start())

    @pl.when(s < sections - 2)
    def _():
        a_start()

    @pl.when(s < sections // 2)
    def _():
        a_middle()

    def chain_copy(m, r):
        return pltpu.make_async_remote_copy(
            src_ref=dx_ref.at[0, m, pl.ds(r * ROWS, ROWS), :],
            dst_ref=dyin.at[m, pl.ds(r * ROWS, ROWS), :],
            send_sem=c_send.at[m, r], recv_sem=c_recv.at[m, r],
            device_id=(s - 1, p), device_id_type=MESH,
        )

    @pl.when(s == sections - 1)
    def _():
        get_c.wait()

    def relay(step, carry):
        m, r = step // per, lax.rem(step, per)

        @pl.when(s < sections - 1)
        def _():
            chain_copy(m, r).wait_recv()

        at = pl.ds(pl.multiple_of(r * ROWS, ROWS), ROWS)
        dy = dyin[m, at, :].astype(f32)
        part = (dy * slope[m, at, :]).astype(bf16)
        dh[pl.ds(pl.multiple_of(step * ROWS, ROWS), ROWS), :] = part
        back = lax.dot_general(
            part, w_ref[...], (((1,), (1,)), ((), ())), preferred_element_type=f32
        )
        dx_ref[0, m, at, :] = (dy + back).astype(bf16)

        @pl.when(s > 0)
        def _():
            chain_copy(m, r).start()

        return carry

    lax.fori_loop(0, micro * per, relay, 0)

    @pl.when(s >= sections - 2)
    def _():
        a_start()

    d = dh[...]
    dt = d.T
    at = 0
    for i in range(nb):
        prod = dot(dt[i * T:(i + 1) * T, :], d[:, i * T:])
        for j in range(nb - i):
            own[(at + j) * T:(at + j + 1) * T, :] = prod[:, j * T:(j + 1) * T]
        at += nb - i
    for i in range(nb):
        prod = dot(xt[i * T:(i + 1) * T, :], d)
        for j in range(nb):
            own[(at + j) * T:(at + j + 1) * T, :] = prod[:, j * T:(j + 1) * T]
        at += nb

    @pl.when(s >= sections // 2)
    def _():
        a_middle()

    def rows_of(chunk, k):
        n, _, first, stride = pieces[k]
        return pl.ds(pl.multiple_of(first + chunk * stride, 16), n)

    def part_of(k):
        n, first, _, _ = pieces[k]
        return slice(first, first + n)

    def slot(k):
        n, first, _, _ = pieces[k]
        return pl.ds(first, n)

    def ring_copy(way, t, k):
        return pltpu.make_async_remote_copy(
            src_ref=stage.at[way, t, slot(k), :], dst_ref=rbuf.at[way, t, slot(k), :],
            send_sem=r_send.at[way, t, k], recv_sem=r_recv.at[way, t, k],
            device_id=(up, down)[way], device_id_type=MESH,
        )

    def ring_send(way, t, k, first):
        chunk = lax.rem(z + half - t if way == 0 else z + half + t, size)
        value = own[rows_of(chunk, k), :]
        if not first:
            ring_copy(way, t - 1, k).wait_recv()
            value = value + rbuf[way, t - 1, part_of(k), :].astype(f32)
        stage[way, t, part_of(k), :] = value.astype(bf16)
        ring_copy(way, t, k).start()

    for k in each:
        ring_send(0, 0, k, True)
        ring_send(1, 1, k, True)
    for k in each:
        ring_send(0, 1, k, False)

    def ring_step(t, carry):
        for k in each:
            for way in range(2):
                ring_send(way, t, k, False)
        return carry

    halves = [slice(h * (width // 2), (h + 1) * (width // 2)) for h in range(2)]

    def newton_first(src):
        at = 0
        for i in range(nb):
            for j in range(i, nb):
                block = src[at * T:(at + 1) * T, :].astype(f32) / count
                if i == j:
                    row = lax.broadcasted_iota(jnp.int32, (T, T), 0)
                    col = lax.broadcasted_iota(jnp.int32, (T, T), 1)
                    block = block + jnp.where(row == col, 0.01, 0.0)
                else:
                    full[j * T:(j + 1) * T, i * T:(i + 1) * T] = block.T
                full[i * T:(i + 1) * T, j * T:(j + 1) * T] = block
                at += 1
        m = full[...]
        inv = 1.0 / jnp.sqrt(jnp.sum(m * m, keepdims=True))
        t = m * inv
        full[...] = t
        tb[0] = t.astype(bf16)
        return inv

    def newton_second():
        for r in halves:
            u = 2.0 * full[r, :] - dot(tb[0, r, :], tb[0])
            ub[0, r, :] = u
            tb[1, r, :] = u.astype(bf16)

    def newton_third():
        for r in halves:
            v = 2.0 * ub[0, r, :] - dot(tb[1, r, :], tb[1])
            ub[1, r, :] = v
            tb[2, r, :] = v.astype(bf16)

    def newton_last(side):
        for r in halves:
            y = 2.0 * (full[r, :] + ub[0, r, :]) - dot(tb[0, r, :], tb[1])
            last = 4.0 * ub[1, r, :] + 2.0 * y - dot(y.astype(bf16), tb[2])
            zb[side, r, :] = last.astype(bf16)

    lax.fori_loop(2, half - 3, ring_step, 0)

    def a_wait(d, carry):
        b_arrived(d).wait_recv()
        return carry

    lax.fori_loop(1, size, a_wait, 0)
    inv_a = newton_first(ared)
    ring_step(half - 3, 0)
    newton_second()
    ring_step(half - 2, 0)
    newton_third()
    ring_step(half - 1, 0)
    newton_last(0)

    def over_copy(k):
        return pltpu.make_async_remote_copy(
            src_ref=xs.at[slot(k), :], dst_ref=xr.at[slot(k), :], send_sem=x_sem.at[0, k],
            recv_sem=x_sem.at[1, k], device_id=over, device_id_type=MESH,
        )

    for k in each:
        value = own[rows_of(z, k), :]
        for way in range(2):
            ring_copy(way, half - 1, k).wait_recv()
            value = value + rbuf[way, half - 1, part_of(k), :].astype(f32)
        xs[part_of(k), :] = value.astype(bf16)
        over_copy(k).start()

    def gather_copy(way, t, k, chunk):
        there = red.at[rows_of(chunk, k), :]
        return pltpu.make_async_remote_copy(
            src_ref=there, dst_ref=there,
            send_sem=g_send.at[way, t, k], recv_sem=g_recv.at[way, t, k],
            device_id=(up, down)[way], device_id_type=MESH,
        )

    def pass_on(way, t, k):
        return gather_copy(way, t, k, lax.rem(z + size - t if way == 0 else z + t, size))

    def arrived(way, t, k):
        return gather_copy(
            way, t, k, lax.rem(z + 2 * size - 1 - t if way == 0 else z + 1 + t, size)
        )

    for k in each:
        over_copy(k).wait_recv()
        total = xs[part_of(k), :].astype(f32) + xr[part_of(k), :].astype(f32)
        red[rows_of(z, k), :] = total.astype(bf16)
        for way in range(2):
            pass_on(way, 0, k).start()

    def gather_step(t, carry):
        for k in each:
            for way in range(2):
                arrived(way, t - 1, k).wait_recv()
                pass_on(way, t, k).start()
        return carry

    lax.fori_loop(1, half - 1, gather_step, 0)
    for k in each:
        arrived(0, half - 2, k).wait_recv()
        pass_on(0, half - 1, k).start()
    arrived(1, half - 2, 0).wait_recv()
    arrived(0, half - 1, 0).wait_recv()

    inv_o = newton_first(red)
    newton_second()
    newton_third()
    newton_last(1)
    for k in each[1:]:
        arrived(1, half - 2, k).wait_recv()
        arrived(0, half - 1, k).wait_recv()
    for i in range(nb):
        for j in range(nb):
            block = red[tri + (i * nb + j) * T:tri + (i * nb + j + 1) * T, :]
            tb[0, i * T:(i + 1) * T, j * T:(j + 1) * T] = block
    scale = inv_a * inv_o
    for r in halves:
        h = 8.0 * tb[0, r, :].astype(f32) - dot(tb[0, r, :], zb[1])
        full[r, :] = h
        tb[1, r, :] = h.astype(bf16)
    for r in halves:
        up_ref[0, r, :] = (8.0 * full[r, :] - dot(zb[0, r, :], tb[1])) * scale

    @pl.when(s > 0)
    def _():
        def left(step, carry):
            chain_copy(step // per, lax.rem(step, per)).wait_send()
            return carry

        lax.fori_loop(0, micro * per, left, 0)

    def drain(t, carry):
        for k in each:
            ring_copy(0, t, k).wait_send()
            pass_on(0, t, k).wait_send()
        return carry

    lax.fori_loop(0, half, drain, 0)

    def drain_down(t, carry):
        for k in each:
            ring_copy(1, t + 1, k).wait_send()
            pass_on(1, t, k).wait_send()
        return carry

    lax.fori_loop(0, half - 1, drain_down, 0)

    def drain_direct(d, carry):
        a_copy(d).wait_send()
        b_copy(d).wait_send()
        return carry

    lax.fori_loop(1, size, drain_direct, 0)
    ax_copy.wait_send()
    for k in each:
        over_copy(k).wait_send()


def body(rings, acts, weights, cot_last):
    sections = lax.axis_size("section")
    size = lax.axis_size("dp") // rings
    _, micro, rows, width = acts.shape
    nb = width // T
    tri = nb * (nb + 1) // 2 * T
    total = tri + nb * nb * T
    piece = total // size
    half = size // 2
    parts = len(pieces_of(width, size))
    vmem = pl.BlockSpec(memory_space=pltpu.VMEM)
    anywhere = pl.BlockSpec(memory_space=pl.ANY)
    bf16, f32 = jnp.bfloat16, jnp.float32
    dma = pltpu.SemaphoreType.DMA
    return pl.pallas_call(
        functools.partial(kernel, sections, rings, size),
        name="relay",
        out_shape=(
            jax.ShapeDtypeStruct((1, micro, rows, width), bf16),
            jax.ShapeDtypeStruct((1, width, width), f32),
        ),
        in_specs=[anywhere] * 3,
        out_specs=(vmem, vmem),
        scratch_shapes=[
            pltpu.VMEM((micro, rows, width), bf16),
            pltpu.VMEM((width, width), bf16),
            pltpu.VMEM((micro, rows, width), f32),
            pltpu.VMEM((width, micro * rows), bf16),
            pltpu.VMEM((micro, rows, width), bf16),
            pltpu.VMEM((micro * rows, width), bf16),
            pltpu.VMEM((total, T), f32),
            pltpu.VMEM((2, half, piece, T), bf16),
            pltpu.VMEM((2, half, piece, T), bf16),
            pltpu.VMEM((total, T), bf16),
            pltpu.VMEM((piece, T), bf16),
            pltpu.VMEM((piece, T), bf16),
            pltpu.VMEM((tri, T), bf16),
            pltpu.VMEM((size, tri // size, T), bf16),
            pltpu.VMEM((tri, T), bf16),
            pltpu.VMEM((tri // size, T), bf16),
            pltpu.VMEM((tri // size, T), bf16),
            pltpu.VMEM((width, width), f32),
            pltpu.VMEM((3, width, width), bf16),
            pltpu.VMEM((2, width, width), f32),
            pltpu.VMEM((2, width, width), bf16),
            dma((3,)),
            dma((micro, rows // ROWS)), dma((micro, rows // ROWS)),
            dma((2, half, parts)), dma((2, half, parts)),
            dma((2, parts)),
            dma((2, half, parts)), dma((2, half, parts)),
            dma((size,)), dma((size,)), dma((size,)), dma((size,)),
            dma((2,)),
        ],
        compiler_params=pltpu.CompilerParams(
            collective_id=0, has_side_effects=True, vmem_limit_bytes=40 << 20
        ),
    )(acts, weights, cot_last)


def solution(mesh):
    placed = (P("section", None, "dp", None), P("section", None, None), P(None, "dp", None))
    return jax.shard_map(
        functools.partial(body, 2),
        mesh=mesh,
        in_specs=placed,
        out_specs=(P("section", None, "dp", None), P("section", None, None)),
        check_vma=False,
    )
```

time: 121 us -> 118 us (0.975)
  the two profiles are of different devices: /device:TPU:32 before, /device:TPU:4 now
where the time goes in v2:
time: 118 us; the launch traced here: 117 us
  Pallas kernels  112 us (95%)
  local copies, waits for them, and re-layouts  4.61 us (4%)
    pallas_call x1, Pallas kernels, body(): pl.pallas_call(functools.partial(kernel, sections, rings, size), name='re...  112 us
    unnamed x8, local copies, waits for them, and re-layouts  4.61 us

profile of v2, /device:TPU:4, one launch (start us, length us, event | category | flops | bytes accessed | tf_op | source)
XLA Modules:
  0.0 117.4 jit_solution(14398910260446395692)
XLA Ops:
  0.6 0.0 copy-start
  0.6 1.0 copy-done
  1.7 0.0 copy-start.1
  1.7 0.9 copy-done.1
  2.6 0.0 copy-start.2
  2.6 0.9 copy-done.2
  3.6 112.1 %relay.1 = (bf16[1,2,128,512]{3,2,1,0:T(8,128)(2,1)S(1)}, f32[1,512,512]{2,1,0:T(8,128)S(1)}) custom-call(bf16[1,2,128,512]{3,2,1,0:T(8,128)(2,1)S(1)} %copy-done.1, bf16[1,512,512]{2,1,0:T(8,128)(2,1)S(1)} %copy-done, bf16[2,128,512]{2,1,0:T(8,128)(2,1)S(1)} %copy-done.2), custom_call_target="tpu_custom_call" | custom-call | tf_op jit(solution)/shard_map/relay/pallas_call | solution.py:425
  115.7 0.7 copy.7
  116.4 1.0 copy.8
Async XLA Ops:
  0.6 1.0 copy-start
  1.7 0.9 copy-start.1
  2.6 0.9 copy-start.2

commit v3 on v0

v3 whole, which is shorter than its diff:
```python
import functools

import jax
import jax.numpy as jnp
from jax import lax
from jax.experimental import pallas as pl
from jax.experimental.pallas import tpu as pltpu
from jax.sharding import PartitionSpec as P

MESH = pl.DeviceIdType.MESH
T = 128
ROWS = 16
STAGES = 4


def dot(a, b):
    return jnp.dot(a, b, preferred_element_type=jnp.float32)


def ring_of(width, size):
    nb = width // T
    tri, square = nb * (nb + 1) // 2 * T, nb * nb * T
    o, g = tri // size, square // size
    return ((o, 0, 0),), ((o, 0, 0), (g, o, tri))


def kernel(
    sections, rings, size,
    acts_hbm, w_hbm, cot_hbm, dx_hbm, up_ref,
    x_ref, w2, x2, slope, xt, dyin, dhl, dxl, rdh, rdx,
    a_own, a_cst, a_crb, a_orb, a_red, a_xs, a_xr,
    b_own, b_cst, b_crb, b_orb, b_red, b_xs, b_xr,
    full, tb, ub, zb, inv,
    in_sem, pair_sem, dh_send, dh_recv, c_send, c_recv,
    a_sem, a_xsem, b_sem, b_xsem,
):
    s = lax.axis_index("section")
    p = lax.axis_index("dp")
    z, ring = lax.rem(p, size), p // size
    base = ring * size
    core, chip = lax.rem(s, 2), s // 2
    chips = sections // 2
    width = w2.shape[1]
    nb = width // T
    tri = nb * (nb + 1) // 2 * T
    rows = dyin.shape[0]
    micro = x_ref.shape[0]
    count = micro * rows * rings * size
    f32, bf16 = jnp.float32, jnp.bfloat16

    def along(d):
        return (s, base + lax.rem(z + size + d, size))

    over = (s, lax.rem(p + size, rings * size))
    partner = (s + 1 - 2 * core, p)

    barrier = pltpu.get_barrier_semaphore()
    peers = (along(1), along(-1), along(2), along(-2), over, partner, (lax.rem(s + 2, sections), p))
    for peer in peers:
        pl.semaphore_signal(barrier, inc=1, device_id=peer, device_id_type=MESH)

    get_x = pltpu.make_async_copy(acts_hbm.at[0], x_ref, in_sem.at[0])
    get_w = pltpu.make_async_copy(w_hbm.at[0], w2.at[core], in_sem.at[1])
    get_c = pltpu.make_async_copy(cot_hbm.at[core], dyin, in_sem.at[2])
    get_x.start()
    get_w.start()

    @pl.when(chip == chips - 1)
    def _():
        get_c.start()

    get_x.wait()
    get_w.wait()
    pl.semaphore_wait(barrier, len(peers))

    def pair_copy(src, dst, i):
        return pltpu.make_async_remote_copy(
            src_ref=src, dst_ref=dst, send_sem=pair_sem.at[0, i], recv_sem=pair_sem.at[1, i],
            device_id=partner, device_id_type=MESH,
        )

    x_copy = pair_copy(x_ref.at[1 - core], x2, 0)
    w_copy = pair_copy(w2.at[core], w2.at[core], 1)
    w_here = pair_copy(w2.at[1 - core], w2.at[1 - core], 1)
    x_copy.start()
    w_copy.start()

    def slope_of(x, which):
        pre = dot(x, w2[which])
        sig = 1.0 / (1.0 + jnp.exp(-pre))
        slope[which] = sig * (1.0 + pre * (1.0 - sig))

    slope_of(x_ref[core], core)
    x_copy.wait_recv()
    w_here.wait_recv()
    slope_of(x2[...], 1 - core)

    def upper(left, right, dst):
        at = 0
        for i in range(nb):
            prod = dot(left[i * T:(i + 1) * T, :], right[:, i * T:]).astype(bf16)
            for j in range(nb - i):
                dst[(at + j) * T:(at + j + 1) * T, :] = prod[:, j * T:(j + 1) * T]
            at += nb - i

    def act_sum():
        x = jnp.concatenate([x_ref[core], x_ref[1 - core]], axis=0)
        xt[...] = x.T
        upper(xt, x, a_own)

    def make_ring(pieces, own, cst, crb, orb, red, xs, xr, sem, xsem):
        each = range(len(pieces))

        def rows_of(chunk, k):
            n, _, first = pieces[k]
            return pl.ds(pl.multiple_of(first + lax.rem(chunk + size, size) * n, 16), n)

        def part(k):
            n, first, _ = pieces[k]
            return slice(first, first + n)

        def slot(k):
            n, first, _ = pieces[k]
            return pl.ds(first, n)

        def copy(kind, src, dst, way, t, k):
            step = (2, 1, 2, 1)[kind]
            return pltpu.make_async_remote_copy(
                src_ref=src, dst_ref=dst,
                send_sem=sem.at[0, kind, way, t, k], recv_sem=sem.at[1, kind, way, t, k],
                device_id=along(step if way == 0 else -step), device_id_type=MESH,
            )

        def sign(way, d):
            return z + d if way == 0 else z - d

        def chain(way, t, k):
            return copy(0, cst.at[way, t, slot(k), :], crb.at[way, t, slot(k), :], way, t, k)

        def odd(way, t, k):
            mine = own.at[rows_of(sign(way, 2 * STAGES - 1 - 2 * t), k), :]
            return copy(1, mine, orb.at[way, t, slot(k), :], way, t, k)

        def spread(kind, way, t, k, chunk):
            there = red.at[rows_of(chunk, k), :]
            return copy(kind, there, there, way, t, k)

        def sent(kind, way, t, k):
            return spread(kind, way, t, k, sign(way, -2 * t))

        def arrived(kind, way, t, k):
            return spread(kind, way, t, k, sign(way, -2 * t - (2, 1)[kind - 2]))

        def across(k):
            return pltpu.make_async_remote_copy(
                src_ref=xs.at[slot(k), :], dst_ref=xr.at[slot(k), :],
                send_sem=xsem.at[0, k], recv_sem=xsem.at[1, k],
                device_id=over, device_id_type=MESH,
            )

        def collect(value, way, t, k, chained):
            odd(way, t, k).wait_recv()
            value = value + orb[way, t, part(k), :].astype(f32)
            if chained:
                chain(way, t, k).wait_recv()
                value = value + crb[way, t, part(k), :].astype(f32)
            return value

        def first():
            for k in each:
                cst[0, 0, part(k), :] = own[rows_of(z + 2 * STAGES, k), :]
                chain(0, 0, k).start()
                for way in range(2):
                    odd(way, 0, k).start()

        def middle(t, chained):
            for k in each:
                for way in range(2):
                    odd(way, t, k).start()
            for k in each:
                for way in range(2):
                    value = own[rows_of(sign(way, 2 * STAGES - 2 * t), k), :].astype(f32)
                    value = collect(value, way, t - 1, k, chained[way])
                    cst[way, t, part(k), :] = value.astype(bf16)
                    chain(way, t, k).start()

        def owner():
            for k in each:
                value = own[rows_of(z, k), :].astype(f32)
                for way in range(2):
                    value = collect(value, way, STAGES - 1, k, True)
                xs[part(k), :] = value.astype(bf16)
                across(k).start()

        def start_gather():
            for k in each:
                across(k).wait_recv()
                total = xs[part(k), :].astype(f32) + xr[part(k), :].astype(f32)
                red[rows_of(z, k), :] = total.astype(bf16)
                for kind in (2, 3):
                    for way in range(2):
                        sent(kind, way, 0, k).start()

        def pass_on(t, ways):
            for k in each:
                for way in range(2):
                    arrived(2, way, t - 1, k).wait_recv()
                    if way in ways:
                        sent(2, way, t, k).start()
                    sent(3, way, t, k).start()

        def stage(t):
            pl.when(t == 0)(first)
            pl.when(t == 1)(lambda: middle(1, (True, False)))
            pl.when(jnp.logical_and(t > 1, t < STAGES))(lambda: middle(t, (True, True)))
            pl.when(t == STAGES)(owner)
            pl.when(t == STAGES + 1)(start_gather)
            pl.when(jnp.logical_and(t > STAGES + 1, t < 2 * STAGES))(
                lambda: pass_on(t - STAGES - 1, (0, 1))
            )
            pl.when(t == 2 * STAGES)(lambda: pass_on(STAGES - 1, (0,)))

        def finish(k):
            for t in range(STAGES):
                for way in range(2):
                    arrived(3, way, t, k).wait_recv()
            arrived(2, 0, STAGES - 1, k).wait_recv()

        def drain():
            for k in each:
                for way in range(2):
                    def left(t, carry):
                        odd(way, t, k).wait_send()
                        sent(3, way, t, k).wait_send()
                        return carry

                    def left_two(t, carry):
                        chain(way, t + way, k).wait_send()
                        sent(2, way, t, k).wait_send()
                        return carry

                    lax.fori_loop(0, STAGES, left, 0)
                    lax.fori_loop(0, STAGES - way, left_two, 0)
                across(k).wait_send()

        return stage, finish, drain

    a_pieces, b_pieces = ring_of(width, size)
    a_stage, a_finish, a_drain = make_ring(
        a_pieces, a_own, a_cst, a_crb, a_orb, a_red, a_xs, a_xr, a_sem, a_xsem
    )
    b_stage, b_finish, b_drain = make_ring(
        b_pieces, b_own, b_cst, b_crb, b_orb, b_red, b_xs, b_xr, b_sem, b_xsem
    )

    ahead = chips - 1 - chip

    def a_ahead(t, carry):
        a_stage(t)
        return carry

    @pl.when(chip < chips - 1)
    def _():
        act_sum()

    lax.fori_loop(0, ahead, a_ahead, 0)

    def chain_copy(r):
        at = pl.ds(pl.multiple_of(r * ROWS, ROWS), ROWS)
        return pltpu.make_async_remote_copy(
            src_ref=dxl.at[0, at, :], dst_ref=dyin.at[at, :],
            send_sem=c_send.at[r], recv_sem=c_recv.at[r],
            device_id=(s - 2, p), device_id_type=MESH,
        )

    def dh_copy(r):
        at = pl.ds(pl.multiple_of(r * ROWS, ROWS), ROWS)
        return pltpu.make_async_remote_copy(
            src_ref=dhl.at[1 - core, at, :], dst_ref=rdh.at[at, :],
            send_sem=dh_send.at[r], recv_sem=dh_recv.at[r],
            device_id=partner, device_id_type=MESH,
        )

    @pl.when(chip == chips - 1)
    def _():
        get_c.wait()

    def relay(r, carry):
        @pl.when(chip < chips - 1)
        def _():
            chain_copy(r).wait_recv()

        at = pl.ds(pl.multiple_of(r * ROWS, ROWS), ROWS)
        dy = dyin[at, :].astype(f32)
        for which in (1, 0):
            part = (dy * slope[which, at, :]).astype(bf16)
            dhl[which, at, :] = part
            back = lax.dot_general(
                part, w2[which], (((1,), (1,)), ((), ())), preferred_element_type=f32
            )
            result = (dy + back).astype(bf16)
            dxl[which, at, :] = result
            dy = result.astype(f32)

        @pl.when(chip > 0)
        def _():
            chain_copy(r).start()

        dh_copy(r).start()
        return carry

    lax.fori_loop(0, rows // ROWS, relay, 0)
    dx_copy = pair_copy(dxl.at[1 - core], rdx, 2)
    dx_copy.start()

    @pl.when(chip == chips - 1)
    def _():
        act_sum()

    def dh_wait(r, carry):
        dh_copy(r).wait_recv()
        return carry

    lax.fori_loop(0, rows // ROWS, dh_wait, 0)
    d = jnp.concatenate([dhl[core], rdh[...]], axis=0)
    upper(d.T, d, b_own)
    for i in range(nb):
        prod = dot(xt[i * T:(i + 1) * T, :], d).astype(bf16)
        for j in range(nb):
            b_own[tri + (i * nb + j) * T:tri + (i * nb + j + 1) * T, :] = prod[:, j * T:(j + 1) * T]

    put_mine = pltpu.make_async_copy(dxl.at[core], dx_hbm.at[0, core], in_sem.at[3])
    put_theirs = pltpu.make_async_copy(rdx, dx_hbm.at[0, 1 - core], in_sem.at[4])

    halves = [slice(h * (width // 2), (h + 1) * (width // 2)) for h in range(2)]

    def newton(src, side):
        at = 0
        for i in range(nb):
            for j in range(i, nb):
                block = src[at * T:(at + 1) * T, :].astype(f32) / count
                if i == j:
                    row = lax.broadcasted_iota(jnp.int32, (T, T), 0)
                    col = lax.broadcasted_iota(jnp.int32, (T, T), 1)
                    block = block + jnp.where(row == col, 0.01, 0.0)
                else:
                    full[j * T:(j + 1) * T, i * T:(i + 1) * T] = block.T
                full[i * T:(i + 1) * T, j * T:(j + 1) * T] = block
                at += 1
        m = full[...]
        scale = 1.0 / jnp.sqrt(jnp.sum(m * m, keepdims=True))
        inv[side] = jnp.broadcast_to(scale, inv.shape[1:])
        t = m * scale
        full[...] = t
        tb[0] = t.astype(bf16)
        for r in halves:
            u = 2.0 * full[r, :] - dot(tb[0, r, :], tb[0])
            ub[0, r, :] = u
            tb[1, r, :] = u.astype(bf16)
        for r in halves:
            v = 2.0 * ub[0, r, :] - dot(tb[1, r, :], tb[1])
            ub[1, r, :] = v
            tb[2, r, :] = v.astype(bf16)
        for r in halves:
            y = 2.0 * (full[r, :] + ub[0, r, :]) - dot(tb[0, r, :], tb[1])
            last = 4.0 * ub[1, r, :] + 2.0 * y - dot(y.astype(bf16), tb[2])
            zb[side, r, :] = last.astype(bf16)

    last = 2 * STAGES
    early = ahead >= STAGES

    def both(t, carry):
        b_stage(t)

        @pl.when(ahead + t <= last)
        def _():
            a_stage(ahead + t)

        @pl.when(jnp.logical_and(early, t == last - 2))
        def _():
            for k in range(len(a_pieces)):
                a_finish(k)
            newton(a_red, 0)

        return carry

    lax.fori_loop(0, last + 1, both, 0)

    @pl.when(jnp.logical_not(early))
    def _():
        for k in range(len(a_pieces)):
            a_finish(k)
        newton(a_red, 0)

    dx_copy.wait_recv()
    put_mine.start()
    put_theirs.start()
    b_finish(0)
    newton(b_red, 1)
    b_finish(1)
    for i in range(nb):
        for j in range(nb):
            block = b_red[tri + (i * nb + j) * T:tri + (i * nb + j + 1) * T, :]
            tb[0, i * T:(i + 1) * T, j * T:(j + 1) * T] = block
    scale = inv[0, 0:1, 0:1] * inv[1, 0:1, 0:1]
    for r in halves:
        h = 8.0 * tb[0, r, :].astype(f32) - dot(tb[0, r, :], zb[1])
        full[r, :] = h
        tb[1, r, :] = h.astype(bf16)
    for r in halves:
        up_ref[0, r, :] = (8.0 * full[r, :] - dot(zb[0, r, :], tb[1])) * scale

    def left(r, carry):
        dh_copy(r).wait_send()
        return carry

    lax.fori_loop(0, rows // ROWS, left, 0)

    @pl.when(chip > 0)
    def _():
        def left(r, carry):
            chain_copy(r).wait_send()
            return carry

        lax.fori_loop(0, rows // ROWS, left, 0)

    a_drain()
    b_drain()
    x_copy.wait_send()
    w_copy.wait_send()
    dx_copy.wait_send()
    put_mine.wait()
    put_theirs.wait()


def body(rings, acts, weights, cot_last):
    sections = lax.axis_size("section")
    size = lax.axis_size("dp") // rings
    _, micro, rows, width = acts.shape
    vmem = pl.BlockSpec(memory_space=pltpu.VMEM)
    hbm = pl.BlockSpec(memory_space=pltpu.HBM)
    bf16, f32 = jnp.bfloat16, jnp.float32
    dma = pltpu.SemaphoreType.DMA

    def ring_scratch(pieces):
        piece = sum(n for n, _, _ in pieces)
        passing = pltpu.VMEM((2, STAGES, piece, T), bf16)
        whole = pltpu.VMEM((piece * size, T), bf16)
        message = pltpu.VMEM((piece, T), bf16)
        return [whole, passing, passing, passing, whole, message, message]

    a_pieces, b_pieces = ring_of(width, size)
    return pl.pallas_call(
        functools.partial(kernel, sections, rings, size),
        name="relay",
        out_shape=(
            jax.ShapeDtypeStruct((1, micro, rows, width), bf16),
            jax.ShapeDtypeStruct((1, width, width), f32),
        ),
        in_specs=[hbm] * 3,
        out_specs=(hbm, vmem),
        scratch_shapes=[
            pltpu.VMEM((micro, rows, width), bf16),
            pltpu.VMEM((2, width, width), bf16),
            pltpu.VMEM((rows, width), bf16),
            pltpu.VMEM((2, rows, width), f32),
            pltpu.VMEM((width, micro * rows), bf16),
            pltpu.VMEM((rows, width), bf16),
            pltpu.VMEM((2, rows, width), bf16),
            pltpu.VMEM((2, rows, width), bf16),
            pltpu.VMEM((rows, width), bf16),
            pltpu.VMEM((rows, width), bf16),
            *ring_scratch(a_pieces),
            *ring_scratch(b_pieces),
            pltpu.VMEM((width, width), f32),
            pltpu.VMEM((3, width, width), bf16),
            pltpu.VMEM((2, width, width), f32),
            pltpu.VMEM((2, width, width), bf16),
            pltpu.VMEM((2, 8, T), f32),
            dma((5,)), dma((2, 3)),
            dma((rows // ROWS,)), dma((rows // ROWS,)),
            dma((rows // ROWS,)), dma((rows // ROWS,)),
            dma((2, 4, 2, STAGES, len(a_pieces))), dma((2, len(a_pieces))),
            dma((2, 4, 2, STAGES, len(b_pieces))), dma((2, len(b_pieces))),
        ],
        compiler_params=pltpu.CompilerParams(
            collective_id=0, has_side_effects=True, vmem_limit_bytes=63 << 20
        ),
    )(acts, weights, cot_last)


def solution(mesh):
    placed = (P("section", None, "dp", None), P("section", None, None), P(None, "dp", None))
    return jax.shard_map(
        functools.partial(body, 2),
        mesh=mesh,
        in_specs=placed,
        out_specs=(P("section", None, "dp", None), P("section", None, None)),
        check_vma=False,
    )
```

time: 501 us -> 92.2 us (0.18)
  the two profiles are of different devices: /device:TPU:8 before, /device:TPU:32 now
where the time goes in v3:
time: 92.2 us; the launch traced here: 92 us
  Pallas kernels  87.4 us (95%)
  local copies, waits for them, and re-layouts  3.93 us (4%)
    pallas_call x1, Pallas kernels, body(): pl.pallas_call(functools.partial(kernel, sections, rings, size), name='re...  87.4 us
    unnamed x2, local copies, waits for them, and re-layouts  3.93 us

profile of v3, /device:TPU:32, one launch (start us, length us, event | category | flops | bytes accessed | tf_op | source)
XLA Modules:
  0.0 92.0 jit_solution(13512548012935027770)
XLA Ops:
  0.6 87.4 %relay.1 = (bf16[1,2,128,512]{3,2,1,0:T(8,128)(2,1)}, f32[1,512,512]{2,1,0:T(8,128)}) custom-call(bf16[1,2,128,512]{3,2,1,0:T(8,128)(2,1)} %acts_hbm.1, bf16[1,512,512]{2,1,0:T(8,128)(2,1)} %w_hbm.1, bf16[2,128,512]{2,1,0:T(8,128)(2,1)} %cot_hbm.1), custom_call_target="tpu_custom_call" | custom-call | tf_op jit(solution)/shard_map/relay/pallas_call | solution.py:453
  88.0 1.7 %copy.7 = bf16[1,2,128,512]{3,2,1,0:T(8,128)(2,1)} copy(bf16[1,2,128,512]{3,2,1,0:T(8,128)(2,1)} %get-tuple-element.4) | data formatting | bytes 524288
  89.7 2.3 %copy.8 = f32[1,512,512]{2,1,0:T(8,128)} copy(f32[1,512,512]{2,1,0:T(8,128)} %get-tuple-element.5) | data formatting | bytes 2097152

commit v4 on v3

--- a/solution.py
+++ b/solution.py
@@ -26,8 +26,8 @@
 
 def kernel(
     sections, rings, size,
-    acts_hbm, w_hbm, cot_hbm, dx_hbm, up_ref,
-    x_ref, w2, x2, slope, xt, dyin, dhl, dxl, rdh, rdx,
+    acts_hbm, w_hbm, cot_hbm, dx_ref, h_ref, za_ref,
+    x_ref, w2, wt, x2, slope, xt, dyin, dhl, dxl, rdh, rdx,
     a_own, a_cst, a_crb, a_orb, a_red, a_xs, a_xr,
     b_own, b_cst, b_crb, b_orb, b_red, b_xs, b_xr,
     full, tb, ub, zb, inv,
@@ -40,6 +40,7 @@
     base = ring * size
     core, chip = lax.rem(s, 2), s // 2
     chips = sections // 2
+    mine = lax.rem(core + chips - 1 - chip, 2)
     width = w2.shape[1]
     nb = width // T
     tri = nb * (nb + 1) // 2 * T
@@ -55,13 +56,13 @@
     partner = (s + 1 - 2 * core, p)
 
     barrier = pltpu.get_barrier_semaphore()
-    peers = (along(1), along(-1), along(2), along(-2), over, partner, (lax.rem(s + 2, sections), p))
+    peers = (along(1), along(-1), along(2), along(-2), over, partner, (2 * lax.rem(chip + 1, chips) + 1 - core, p))
     for peer in peers:
         pl.semaphore_signal(barrier, inc=1, device_id=peer, device_id_type=MESH)
 
     get_x = pltpu.make_async_copy(acts_hbm.at[0], x_ref, in_sem.at[0])
     get_w = pltpu.make_async_copy(w_hbm.at[0], w2.at[core], in_sem.at[1])
-    get_c = pltpu.make_async_copy(cot_hbm.at[core], dyin, in_sem.at[2])
+    get_c = pltpu.make_async_copy(cot_hbm.at[mine], dyin, in_sem.at[2])
     get_x.start()
     get_w.start()
 
@@ -79,7 +80,7 @@
             device_id=partner, device_id_type=MESH,
         )
 
-    x_copy = pair_copy(x_ref.at[1 - core], x2, 0)
+    x_copy = pair_copy(x_ref.at[1 - mine], x2, 0)
     w_copy = pair_copy(w2.at[core], w2.at[core], 1)
     w_here = pair_copy(w2.at[1 - core], w2.at[1 - core], 1)
     x_copy.start()
@@ -90,10 +91,12 @@
         sig = 1.0 / (1.0 + jnp.exp(-pre))
         slope[which] = sig * (1.0 + pre * (1.0 - sig))
 
-    slope_of(x_ref[core], core)
+    slope_of(x_ref[mine], core)
+    wt[core] = w2[core].T
     x_copy.wait_recv()
     w_here.wait_recv()
     slope_of(x2[...], 1 - core)
+    wt[1 - core] = w2[1 - core].T
 
     def upper(left, right, dst):
         at = 0
@@ -104,7 +107,7 @@
             at += nb - i
 
     def act_sum():
-        x = jnp.concatenate([x_ref[core], x_ref[1 - core]], axis=0)
+        x = jnp.concatenate([x_ref[mine], x_ref[1 - mine]], axis=0)
         xt[...] = x.T
         upper(xt, x, a_own)
 
@@ -166,12 +169,15 @@
                 value = value + crb[way, t, part(k), :].astype(f32)
             return value
 
-        def first():
-            for k in each:
-                cst[0, 0, part(k), :] = own[rows_of(z + 2 * STAGES, k), :]
-                chain(0, 0, k).start()
-                for way in range(2):
-                    odd(way, 0, k).start()
+        def first(k):
+            cst[0, 0, part(k), :] = own[rows_of(z + 2 * STAGES, k), :]
+            chain(0, 0, k).start()
+            for way in range(2):
+                odd(way, 0, k).start()
+
+        def all_first():
+            for k in each:
+                first(k)
 
         def middle(t, chained):
             for k in each:
@@ -209,8 +215,9 @@
                         sent(2, way, t, k).start()
                     sent(3, way, t, k).start()
 
-        def stage(t):
-            pl.when(t == 0)(first)
+        def stage(t, begun=False):
+            if not begun:
+                pl.when(t == 0)(all_first)
             pl.when(t == 1)(lambda: middle(1, (True, False)))
             pl.when(jnp.logical_and(t > 1, t < STAGES))(lambda: middle(t, (True, True)))
             pl.when(t == STAGES)(owner)
@@ -243,13 +250,13 @@
                     lax.fori_loop(0, STAGES - way, left_two, 0)
                 across(k).wait_send()
 
-        return stage, finish, drain
+        return first, stage, finish, drain
 
     a_pieces, b_pieces = ring_of(width, size)
-    a_stage, a_finish, a_drain = make_ring(
+    _, a_stage, a_finish, a_drain = make_ring(
         a_pieces, a_own, a_cst, a_crb, a_orb, a_red, a_xs, a_xr, a_sem, a_xsem
     )
-    b_stage, b_finish, b_drain = make_ring(
+    b_first, b_stage, b_finish, b_drain = make_ring(
         b_pieces, b_own, b_cst, b_crb, b_orb, b_red, b_xs, b_xr, b_sem, b_xsem
     )
 
@@ -270,7 +277,7 @@
         return pltpu.make_async_remote_copy(
             src_ref=dxl.at[0, at, :], dst_ref=dyin.at[at, :],
             send_sem=c_send.at[r], recv_sem=c_recv.at[r],
-            device_id=(s - 2, p), device_id_type=MESH,
+            device_id=(2 * chip - 1 - core, p), device_id_type=MESH,
         )
 
     def dh_copy(r):
@@ -295,10 +302,7 @@
         for which in (1, 0):
             part = (dy * slope[which, at, :]).astype(bf16)
             dhl[which, at, :] = part
-            back = lax.dot_general(
-                part, w2[which], (((1,), (1,)), ((), ())), preferred_element_type=f32
-            )
-            result = (dy + back).astype(bf16)
+            result = (dy + dot(part, wt[which])).astype(bf16)
             dxl[which, at, :] = result
             dy = result.astype(f32)
 
@@ -324,17 +328,19 @@
     lax.fori_loop(0, rows // ROWS, dh_wait, 0)
     d = jnp.concatenate([dhl[core], rdh[...]], axis=0)
     upper(d.T, d, b_own)
+    b_first(0)
     for i in range(nb):
         prod = dot(xt[i * T:(i + 1) * T, :], d).astype(bf16)
         for j in range(nb):
             b_own[tri + (i * nb + j) * T:tri + (i * nb + j + 1) * T, :] = prod[:, j * T:(j + 1) * T]
-
-    put_mine = pltpu.make_async_copy(dxl.at[core], dx_hbm.at[0, core], in_sem.at[3])
-    put_theirs = pltpu.make_async_copy(rdx, dx_hbm.at[0, 1 - core], in_sem.at[4])
+    b_first(1)
+
+    put_mine = pltpu.make_async_copy(dxl.at[core], dx_ref.at[0, mine], in_sem.at[3])
+    put_theirs = pltpu.make_async_copy(rdx, dx_ref.at[0, 1 - mine], in_sem.at[4])
 
     halves = [slice(h * (width // 2), (h + 1) * (width // 2)) for h in range(2)]
 
-    def newton(src, side):
+    def newton(src, side, dst):
         at = 0
         for i in range(nb):
             for j in range(i, nb):
@@ -364,23 +370,23 @@
         for r in halves:
             y = 2.0 * (full[r, :] + ub[0, r, :]) - dot(tb[0, r, :], tb[1])
             last = 4.0 * ub[1, r, :] + 2.0 * y - dot(y.astype(bf16), tb[2])
-            zb[side, r, :] = last.astype(bf16)
+            dst[r, :] = last.astype(bf16)
 
     last = 2 * STAGES
-    early = ahead >= STAGES
+    early = ahead > STAGES
 
     def both(t, carry):
-        b_stage(t)
+        b_stage(t, True)
 
         @pl.when(ahead + t <= last)
         def _():
             a_stage(ahead + t)
 
-        @pl.when(jnp.logical_and(early, t == last - 2))
+        @pl.when(jnp.logical_and(early, t == STAGES))
         def _():
             for k in range(len(a_pieces)):
                 a_finish(k)
-            newton(a_red, 0)
+            newton(a_red, 0, za_ref)
 
         return carry
 
@@ -390,13 +396,13 @@
     def _():
         for k in range(len(a_pieces)):
             a_finish(k)
-        newton(a_red, 0)
+        newton(a_red, 0, za_ref)
 
     dx_copy.wait_recv()
     put_mine.start()
     put_theirs.start()
     b_finish(0)
-    newton(b_red, 1)
+    newton(b_red, 1, zb)
     b_finish(1)
     for i in range(nb):
         for j in range(nb):
@@ -404,11 +410,7 @@
             tb[0, i * T:(i + 1) * T, j * T:(j + 1) * T] = block
     scale = inv[0, 0:1, 0:1] * inv[1, 0:1, 0:1]
     for r in halves:
-        h = 8.0 * tb[0, r, :].astype(f32) - dot(tb[0, r, :], zb[1])
-        full[r, :] = h
-        tb[1, r, :] = h.astype(bf16)
-    for r in halves:
-        up_ref[0, r, :] = (8.0 * full[r, :] - dot(zb[0, r, :], tb[1])) * scale
+        h_ref[r, :] = (8.0 * tb[0, r, :].astype(f32) - dot(tb[0, r, :], zb[...])) * scale
 
     def left(r, carry):
         dh_copy(r).wait_send()
@@ -431,6 +433,22 @@
     dx_copy.wait_send()
     put_mine.wait()
     put_theirs.wait()
+
+
+def finish_kernel(dx_ref, h_ref, za_ref, dx_hbm, up_hbm, up, sem):
+    put_dx = pltpu.make_async_copy(dx_ref, dx_hbm, sem.at[0])
+    put_dx.start()
+    h = h_ref[...].astype(jnp.bfloat16)
+    puts = []
+    for i in range(up.shape[0] // T):
+        r = slice(i * T, (i + 1) * T)
+        up[r, :] = 8.0 * h_ref[r, :] - dot(za_ref[r, :], h)
+        put = pltpu.make_async_copy(up.at[r, :], up_hbm.at[0, r, :], sem.at[1 + i])
+        put.start()
+        puts.append(put)
+    put_dx.wait()
+    for put in puts:
+        put.wait()
 
 
 def body(rings, acts, weights, cot_last):
@@ -450,17 +468,19 @@
         return [whole, passing, passing, passing, whole, message, message]
 
     a_pieces, b_pieces = ring_of(width, size)
-    return pl.pallas_call(
+    dx, h, za = pl.pallas_call(
         functools.partial(kernel, sections, rings, size),
         name="relay",
         out_shape=(
             jax.ShapeDtypeStruct((1, micro, rows, width), bf16),
-            jax.ShapeDtypeStruct((1, width, width), f32),
+            jax.ShapeDtypeStruct((width, width), f32),
+            jax.ShapeDtypeStruct((width, width), bf16),
         ),
         in_specs=[hbm] * 3,
-        out_specs=(hbm, vmem),
+        out_specs=(vmem, vmem, vmem),
         scratch_shapes=[
             pltpu.VMEM((micro, rows, width), bf16),
+            pltpu.VMEM((2, width, width), bf16),
             pltpu.VMEM((2, width, width), bf16),
             pltpu.VMEM((rows, width), bf16),
             pltpu.VMEM((2, rows, width), f32),
@@ -475,7 +495,7 @@
             pltpu.VMEM((width, width), f32),
             pltpu.VMEM((3, width, width), bf16),
             pltpu.VMEM((2, width, width), f32),
-            pltpu.VMEM((2, width, width), bf16),
+            pltpu.VMEM((width, width), bf16),
             pltpu.VMEM((2, 8, T), f32),
             dma((5,)), dma((2, 3)),
             dma((rows // ROWS,)), dma((rows // ROWS,)),
@@ -484,9 +504,24 @@
             dma((2, 4, 2, STAGES, len(b_pieces))), dma((2, len(b_pieces))),
         ],
         compiler_params=pltpu.CompilerParams(
-            collective_id=0, has_side_effects=True, vmem_limit_bytes=63 << 20
+            collective_id=0, has_side_effects=True, vmem_limit_bytes=48 << 20
         ),
-    )(acts, weights, cot_last)
+    )(*(pltpu.with_memory_space_constraint(a, pltpu.HBM) for a in (acts, weights, cot_last)))
+    return pl.pallas_call(
+        finish_kernel,
+        name="finish",
+        out_shape=(
+            jax.ShapeDtypeStruct((1, micro, rows, width), bf16),
+            jax.ShapeDtypeStruct((1, width, width), f32),
+        ),
+        in_specs=[vmem] * 3,
+        out_specs=(hbm, hbm),
+        scratch_shapes=[
+            pltpu.VMEM((width, width), f32),
+            dma((1 + width // T,)),
+        ],
+        compiler_params=pltpu.CompilerParams(vmem_limit_bytes=8 << 20),
+    )(dx, h, za)
 
 
 def solution(mesh):

time: 92.2 us -> 86 us (0.933)
  the two profiles are of different devices: /device:TPU:32 before, /device:TPU:1 now
where the time goes in v4:
time: 86 us; the launch traced here: 85.8 us
  Pallas kernels  85.2 us (99%)
    pallas_call x1, Pallas kernels, body(): pl.pallas_call(functools.partial(kernel, sections, rings, size), name='re...  84 us

profile of v4, /device:TPU:1, one launch (start us, length us, event | category | flops | bytes accessed | tf_op | source)
XLA Modules:
  0.0 85.8 jit_solution(472805059289779550)
XLA Ops:
  0.6 84.0 %relay.1 = (bf16[1,2,128,512]{3,2,1,0:T(8,128)(2,1)S(1)}, f32[512,512]{1,0:T(8,128)S(1)}, bf16[512,512]{1,0:T(8,128)(2,1)S(1)}) custom-call(bf16[1,2,128,512]{3,2,1,0:T(8,128)(2,1)} %acts_hbm.1, bf16[1,512,512]{2,1,0:T(8,128)(2,1)} %w_hbm.1, bf16[2,128,512]{2,1,0:T(8,128)(2,1)} %cot_hbm.1), custom_call_target="tpu_custom_call" | custom-call | tf_op jit(solution)/shard_map/relay/pallas_call | solution.py:471
  84.6 1.2 %finish.1 = (bf16[1,2,128,512]{3,2,1,0:T(8,128)(2,1)}, f32[1,512,512]{2,1,0:T(8,128)}) custom-call(bf16[1,2,128,512]{3,2,1,0:T(8,128)(2,1)S(1)} %get-tuple-element.5.dx_ref, f32[512,512]{1,0:T(8,128)S(1)} %get-tuple-element.6.h_ref, bf16[512,512]{1,0:T(8,128)(2,1)S(1)} %get-tuple-element.7.za_ref), custom_call_target="tpu_custom_call" | custom-call | tf_op jit(solution)/shard_map/finish/pallas_call | solution.py:510

commit v5 on v4

--- a/solution.py
+++ b/solution.py
@@ -260,7 +260,7 @@
         b_pieces, b_own, b_cst, b_crb, b_orb, b_red, b_xs, b_xr, b_sem, b_xsem
     )
 
-    ahead = chips - 1 - chip
+    ahead = (chips - 1 - chip) * 4 // 7
 
     def a_ahead(t, carry):
         a_stage(t)
@@ -342,25 +342,26 @@
 
     def newton(src, side, dst):
         at = 0
+        squares = jnp.zeros((T, T), f32)
         for i in range(nb):
             for j in range(i, nb):
-                block = src[at * T:(at + 1) * T, :].astype(f32) / count
+                block = src[at * T:(at + 1) * T, :].astype(f32) * (1.0 / count)
                 if i == j:
                     row = lax.broadcasted_iota(jnp.int32, (T, T), 0)
                     col = lax.broadcasted_iota(jnp.int32, (T, T), 1)
                     block = block + jnp.where(row == col, 0.01, 0.0)
+                    squares = squares + block * block
                 else:
                     full[j * T:(j + 1) * T, i * T:(i + 1) * T] = block.T
+                    squares = squares + 2.0 * (block * block)
                 full[i * T:(i + 1) * T, j * T:(j + 1) * T] = block
                 at += 1
-        m = full[...]
-        scale = 1.0 / jnp.sqrt(jnp.sum(m * m, keepdims=True))
+        scale = 1.0 / jnp.sqrt(jnp.sum(squares, keepdims=True))
         inv[side] = jnp.broadcast_to(scale, inv.shape[1:])
-        t = m * scale
-        full[...] = t
-        tb[0] = t.astype(bf16)
+        tb[0] = (full[...] * scale).astype(bf16)
+        twice = 2.0 * scale
         for r in halves:
-            u = 2.0 * full[r, :] - dot(tb[0, r, :], tb[0])
+            u = twice * full[r, :] - dot(tb[0, r, :], tb[0])
             ub[0, r, :] = u
             tb[1, r, :] = u.astype(bf16)
         for r in halves:
@@ -368,12 +369,12 @@
             ub[1, r, :] = v
             tb[2, r, :] = v.astype(bf16)
         for r in halves:
-            y = 2.0 * (full[r, :] + ub[0, r, :]) - dot(tb[0, r, :], tb[1])
+            y = twice * full[r, :] + 2.0 * ub[0, r, :] - dot(tb[0, r, :], tb[1])
             last = 4.0 * ub[1, r, :] + 2.0 * y - dot(y.astype(bf16), tb[2])
             dst[r, :] = last.astype(bf16)
 
     last = 2 * STAGES
-    early = ahead > STAGES
+    early = ahead >= STAGES
 
     def both(t, carry):
         b_stage(t, True)
@@ -382,7 +383,7 @@
         def _():
             a_stage(ahead + t)
 
-        @pl.when(jnp.logical_and(early, t == STAGES))
+        @pl.when(jnp.logical_and(early, t == last - 2))
         def _():
             for k in range(len(a_pieces)):
                 a_finish(k)
@@ -404,13 +405,14 @@
     b_finish(0)
     newton(b_red, 1, zb)
     b_finish(1)
-    for i in range(nb):
-        for j in range(nb):
-            block = b_red[tri + (i * nb + j) * T:tri + (i * nb + j + 1) * T, :]
-            tb[0, i * T:(i + 1) * T, j * T:(j + 1) * T] = block
     scale = inv[0, 0:1, 0:1] * inv[1, 0:1, 0:1]
     for r in halves:
-        h_ref[r, :] = (8.0 * tb[0, r, :].astype(f32) - dot(tb[0, r, :], zb[...])) * scale
+        strips = []
+        for i in range(r.start // T, r.stop // T):
+            blocks = [tri + (i * nb + j) * T for j in range(nb)]
+            strips.append(jnp.concatenate([b_red[at:at + T, :] for at in blocks], axis=1))
+        g = jnp.concatenate(strips, axis=0)
+        h_ref[r, :] = (8.0 * g.astype(f32) - dot(g, zb[...])) * scale
 
     def left(r, carry):
         dh_copy(r).wait_send()

time: 86 us -> 85.7 us (level)
  the two profiles are of different devices: /device:TPU:1 before, /device:TPU:32 now
where the time goes in v5:
time: 85.7 us; the launch traced here: 85.6 us
  Pallas kernels  85 us (99%)
    pallas_call x1, Pallas kernels, body(): pl.pallas_call(functools.partial(kernel, sections, rings, size), name='re...  83.7 us

profile of v5, /device:TPU:32, one launch (start us, length us, event | category | flops | bytes accessed | tf_op | source)
XLA Modules:
  0.0 85.6 jit_solution(5826983153764298046)
XLA Ops:
  0.6 83.7 %relay.1 = (bf16[1,2,128,512]{3,2,1,0:T(8,128)(2,1)S(1)}, f32[512,512]{1,0:T(8,128)S(1)}, bf16[512,512]{1,0:T(8,128)(2,1)S(1)}) custom-call(bf16[1,2,128,512]{3,2,1,0:T(8,128)(2,1)} %acts_hbm.1, bf16[1,512,512]{2,1,0:T(8,128)(2,1)} %w_hbm.1, bf16[2,128,512]{2,1,0:T(8,128)(2,1)} %cot_hbm.1), custom_call_target="tpu_custom_call" | custom-call | tf_op jit(solution)/shard_map/relay/pallas_call | solution.py:473
  84.4 1.2 %finish.1 = (bf16[1,2,128,512]{3,2,1,0:T(8,128)(2,1)}, f32[1,512,512]{2,1,0:T(8,128)}) custom-call(bf16[1,2,128,512]{3,2,1,0:T(8,128)(2,1)S(1)} %get-tuple-element.5.dx_ref, f32[512,512]{1,0:T(8,128)S(1)} %get-tuple-element.6.h_ref, bf16[512,512]{1,0:T(8,128)(2,1)S(1)} %get-tuple-element.7.za_ref), custom_call_target="tpu_custom_call" | custom-call | tf_op jit(solution)/shard_map/finish/pallas_call | solution.py:512

commit v6 on v5

--- a/solution.py
+++ b/solution.py
@@ -402,6 +402,26 @@
     dx_copy.wait_recv()
     put_mine.start()
     put_theirs.start()
+    def left(r, carry):
+        dh_copy(r).wait_send()
+        return carry
+
+    lax.fori_loop(0, rows // ROWS, left, 0)
+
+    @pl.when(chip > 0)
+    def _():
+        def left(r, carry):
+            chain_copy(r).wait_send()
+            return carry
+
+        lax.fori_loop(0, rows // ROWS, left, 0)
+
+    a_drain()
+    b_drain()
+    x_copy.wait_send()
+    w_copy.wait_send()
+    dx_copy.wait_send()
+
     b_finish(0)
     newton(b_red, 1, zb)
     b_finish(1)
@@ -414,25 +434,6 @@
         g = jnp.concatenate(strips, axis=0)
         h_ref[r, :] = (8.0 * g.astype(f32) - dot(g, zb[...])) * scale
 
-    def left(r, carry):
-        dh_copy(r).wait_send()
-        return carry
-
-    lax.fori_loop(0, rows // ROWS, left, 0)
-
-    @pl.when(chip > 0)
-    def _():
-        def left(r, carry):
-            chain_copy(r).wait_send()
-            return carry
-
-        lax.fori_loop(0, rows // ROWS, left, 0)
-
-    a_drain()
-    b_drain()
-    x_copy.wait_send()
-    w_copy.wait_send()
-    dx_copy.wait_send()
     put_mine.wait()
     put_theirs.wait()
 

time: 85.7 us -> 85.3 us (level)
  no operation moved by 1% of the time
where the time goes in v6:
time: 85.3 us; the launch traced here: 85.2 us
  Pallas kernels  84.6 us (99%)
    pallas_call x1, Pallas kernels, body(): pl.pallas_call(functools.partial(kernel, sections, rings, size), name='re...  83.3 us

profile of v6, /device:TPU:32, one launch (start us, length us, event | category | flops | bytes accessed | tf_op | source)
XLA Modules:
  0.0 85.2 jit_solution(10216487483641275032)
XLA Ops:
  0.6 83.3 %relay.1 = (bf16[1,2,128,512]{3,2,1,0:T(8,128)(2,1)S(1)}, f32[512,512]{1,0:T(8,128)S(1)}, bf16[512,512]{1,0:T(8,128)(2,1)S(1)}) custom-call(bf16[1,2,128,512]{3,2,1,0:T(8,128)(2,1)} %acts_hbm.1, bf16[1,512,512]{2,1,0:T(8,128)(2,1)} %w_hbm.1, bf16[2,128,512]{2,1,0:T(8,128)(2,1)} %cot_hbm.1), custom_call_target="tpu_custom_call" | custom-call | tf_op jit(solution)/shard_map/relay/pallas_call | solution.py:474
  83.9 1.2 %finish.1 = (bf16[1,2,128,512]{3,2,1,0:T(8,128)(2,1)}, f32[1,512,512]{2,1,0:T(8,128)}) custom-call(bf16[1,2,128,512]{3,2,1,0:T(8,128)(2,1)S(1)} %get-tuple-element.5.dx_ref, f32[512,512]{1,0:T(8,128)S(1)} %get-tuple-element.6.h_ref, bf16[512,512]{1,0:T(8,128)(2,1)S(1)} %get-tuple-element.7.za_ref), custom_call_target="tpu_custom_call" | custom-call | tf_op jit(solution)/shard_map/finish/pallas_call | solution.py:513

commit v7 on v6

--- a/solution.py
+++ b/solution.py
@@ -277,7 +277,8 @@
         return pltpu.make_async_remote_copy(
             src_ref=dxl.at[0, at, :], dst_ref=dyin.at[at, :],
             send_sem=c_send.at[r], recv_sem=c_recv.at[r],
-            device_id=(2 * chip - 1 - core, p), device_id_type=MESH,
+            device_id=(lax.rem(2 * chip + sections - 1 - core, sections), p),
+            device_id_type=MESH,
         )
 
     def dh_copy(r):

time: 85.3 us -> 85.3 us (level)
  no operation moved by 1% of the time
where the time goes in v7:
time: 85.3 us; the launch traced here: 85.2 us
  Pallas kernels  84.6 us (99%)
    pallas_call x1, Pallas kernels, body(): pl.pallas_call(functools.partial(kernel, sections, rings, size), name='re...  83.3 us

profile of v7, /device:TPU:32, one launch (start us, length us, event | category | flops | bytes accessed | tf_op | source)
XLA Modules:
  0.0 85.2 jit_solution(11935290023488166940)
XLA Ops:
  0.6 83.3 %relay.1 = (bf16[1,2,128,512]{3,2,1,0:T(8,128)(2,1)S(1)}, f32[512,512]{1,0:T(8,128)S(1)}, bf16[512,512]{1,0:T(8,128)(2,1)S(1)}) custom-call(bf16[1,2,128,512]{3,2,1,0:T(8,128)(2,1)} %acts_hbm.1, bf16[1,512,512]{2,1,0:T(8,128)(2,1)} %w_hbm.1, bf16[2,128,512]{2,1,0:T(8,128)(2,1)} %cot_hbm.1), custom_call_target="tpu_custom_call" | custom-call | tf_op jit(solution)/shard_map/relay/pallas_call | solution.py:475
  83.9 1.2 %finish.1 = (bf16[1,2,128,512]{3,2,1,0:T(8,128)(2,1)}, f32[1,512,512]{2,1,0:T(8,128)}) custom-call(bf16[1,2,128,512]{3,2,1,0:T(8,128)(2,1)S(1)} %get-tuple-element.5.dx_ref, f32[512,512]{1,0:T(8,128)S(1)} %get-tuple-element.6.h_ref, bf16[512,512]{1,0:T(8,128)(2,1)S(1)} %get-tuple-element.7.za_ref), custom_call_target="tpu_custom_call" | custom-call | tf_op jit(solution)/shard_map/finish/pallas_call | solution.py:514
